TPU v7x, 256 devices: a whole 4x4x8 slice. The times are simulated.
256 devices in a mesh: nodes: 128 (over y, z, x), params: 2 (over core).
Axes of the slice: x: 4, y: 4, z: 8, core: 2. Of those that a mesh axis runs over, the one named last changes fastest.
Arguments:
- snapshots: bfloat16 [128, 48, 131072], P('params', None, 'nodes'), may hold values from -6 to 6
- space_start: float32 [64, 131072], P(None, 'nodes'), may hold values from -12 to 12
- time_start: float32 [64, 48], replicated, may hold values from -0.9 to 0.9
Outputs:
- space_factor: float32 [64, 131072], P(None, 'nodes')
- param_factor: float32 [64, 128], P(None, 'params')
- time_factor: float32 [64, 48], replicated
All inputs are finite; a program needn't handle non-finite values.
Results may differ from a plain program's by a relative error of at most 0.0093.
Values sent between devices are 32-bit elements; how exact they have to be, the bound alone decides.
No kernel may reach another device: no remote copies, remote signals or barrier semaphores. Data moves between devices by JAX's collectives and lax.ppermute only.
A program may use at most 64 MiB of HBM per device.

v0:
```python
import functools

import jax
import jax.numpy as jnp
from jax import lax
from jax.experimental import pallas as pl
from jax.experimental.pallas import tpu as pltpu
from jax.sharding import Mesh
from jax.sharding import PartitionSpec as P

SWEEPS = 4
NODES = ("nodes_0", "nodes_1", "nodes_2")
PLANE = ("nodes_0", "nodes_2")
LINE = "nodes_1"
CORE = "params"
GROUP = 8
GROUPS = 2
F32 = jnp.float32
BF16 = jnp.bfloat16
EXACT = lax.Precision.HIGHEST
RIDGE_SHARE = 0.01


def dot(a, b, over, precision=None):
    return lax.dot_general(
        a, b, (((over[0],), (over[1],)), ((), ())), precision=precision, preferred_element_type=F32
    )


def gram_rows(a):
    return dot(a, a, (0, 0), EXACT)


def row_of(x, i):
    return jnp.broadcast_to(x[i : i + 1, :], (8, x.shape[1]))


def column_of(x, i):
    return jnp.broadcast_to(x[:, i : i + 1], x.shape)


def eliminate(blocks):
    blocks = list(blocks)
    count = len(blocks)
    sub = lax.broadcasted_iota(jnp.int32, blocks[0].shape, 0)
    for k in range(count):
        lead = [column_of(blocks[k], 8 * k + i) for i in range(8)]
        others = {m: [column_of(blocks[m], 8 * k + i) for i in range(8)] for m in range(count) if m != k}
        rows = blocks[k]
        for i in range(8):
            pivot = sub == i
            factor = jnp.where(pivot, -1.0, lead[i]) * (1.0 / row_of(lead[i], i))
            rows = jnp.where(pivot, 0.0, rows) - factor * row_of(rows, i)
            for n in range(i + 1, 8):
                lead[n] = jnp.where(pivot, 0.0, lead[n]) - factor * row_of(lead[n], i)
        pivots = [row_of(rows, i) for i in range(8)]
        blocks[k] = rows
        for m, columns in others.items():
            terms = [columns[i] * pivots[i] for i in range(8)]
            while len(terms) > 1:
                terms = [terms[i] + terms[i + 1] for i in range(0, len(terms), 2)]
            blocks[m] = blocks[m] - terms[0]
    return blocks


def ridge_inverse(gram):
    n = gram.shape[0]
    row = lax.broadcasted_iota(jnp.int32, (n, n), 0)
    column = lax.broadcasted_iota(jnp.int32, (n, n), 1)
    eye = jnp.where(row == column, 1.0, 0.0).astype(F32)
    trace = jnp.sum(jnp.sum(gram * eye, axis=0, keepdims=True), axis=1, keepdims=True)
    matrix = gram + (RIDGE_SHARE / n) * trace * eye
    both = jnp.concatenate([matrix, eye], axis=1)
    done = eliminate([both[8 * m : 8 * m + 8, :] for m in range(n // 8)])
    return jnp.concatenate(done, axis=0)[:, n:]


def fold(x):
    half = x.shape[0] // 2
    return jnp.concatenate([x[:half, :], x[half:, :]], axis=1)


def unfold(x):
    half = x.shape[1] // 2
    return jnp.concatenate([x[:, :half], x[:, half:]], axis=0)


def total(parts):
    whole = [parts[i] for i in range(parts.shape[0])]
    while len(whole) > 1:
        whole = [whole[i] + whole[i + 1] for i in range(0, len(whole), 2)]
    return whole[0]


def spread(ref, x, rows=slice(None)):
    for i in range(ref.shape[0]):
        ref[i, rows, :] = x


def contract(rows_ref, space, times, contracted_ref, message_ref, side_ref, arrive=None):
    steps, rank = times.shape
    samples = side_ref.shape[0]
    low = space.astype(BF16)
    spread(message_ref, fold(dot(space, space, (1, 1), EXACT)), slice(samples // 2, None))

    def groups(step, carry):
        if arrive is not None:
            arrive(step)
        for group in range(GROUPS):
            first = pl.multiple_of((step * GROUPS + group) * GROUP, GROUP)
            here = pl.ds(pl.multiple_of(first * steps, GROUP * steps), GROUP * steps)
            part = dot(rows_ref[here, :], low, (1, 1))
            contracted_ref[here, :] = part
            sides = [
                jnp.sum(part[j * steps : (j + 1) * steps, :] * times, axis=0, keepdims=True) for j in range(GROUP)
            ]
            side_ref[pl.ds(first, GROUP), :] = jnp.concatenate(sides, axis=0)
        return carry

    lax.fori_loop(0, samples // (GROUP * GROUPS), groups, 0)
    spread(message_ref, fold(side_ref[...]), slice(0, samples // 2))


def start_kernel(
    source_ref, space_ref, times_ref, rows_ref, contracted_ref, message_ref, side_ref, space_here, times_here, arrived, early
):
    count = arrived.shape[0]
    size = rows_ref.shape[0] // count
    others = [
        pltpu.make_async_copy(space_ref, space_here, early.at[0]),
        pltpu.make_async_copy(times_ref, times_here, early.at[1]),
    ]
    for copy in others:
        copy.start()

    def load(i):
        here = pl.ds(pl.multiple_of(i * size, size), size)
        return pltpu.make_async_copy(source_ref.at[here, :], rows_ref.at[here, :], arrived.at[i])

    for i in range(count):
        load(i).start()
    for copy in others:
        copy.wait()
    contract(
        rows_ref, space_here[...], times_here[...], contracted_ref, message_ref, side_ref, lambda step: load(step).wait()
    )


def space_kernel(rows_ref, own_ref, other_ref, inverse_ref, times_ref, contracted_ref, message_ref, side_ref):
    space = dot(inverse_ref[...], own_ref[...] + other_ref[...], (1, 0), EXACT)
    contract(rows_ref, space, times_ref[...], contracted_ref, message_ref, side_ref)


def last_kernel(own_ref, other_ref, inverse_ref, space_ref):
    space_ref[...] = dot(inverse_ref[...], own_ref[...] + other_ref[...], (1, 0), EXACT)


def relay_kernel(parts_ref, copies_ref):
    spread(copies_ref, total(parts_ref))


def pair_kernel(own_ref, other_ref, copies_ref):
    spread(copies_ref, own_ref[...] + other_ref[...])


def params_kernel(parts_ref, times_ref, params_ref, gram_ref, space_gram_ref):
    half = params_ref.shape[0] // 2
    whole = total(parts_ref)
    side, space_gram = unfold(whole[:half, :]), unfold(whole[half:, :])
    space_gram_ref[...] = space_gram
    inverse = ridge_inverse(space_gram * gram_rows(times_ref[...]))
    params = dot(side, inverse, (1, 0), EXACT)
    params_ref[...] = params
    gram_ref[...] = fold(gram_rows(params))


def time_side_kernel(contracted_ref, params_ref, side_ref):
    samples, rank = params_ref.shape
    steps = 2 * side_ref.shape[0]
    sums = [jnp.zeros((8, rank), F32) for _ in range(steps // 8)]
    for j in range(samples):
        factor = jnp.broadcast_to(params_ref[j : j + 1, :], (8, rank))
        for q in range(steps // 8):
            sums[q] = sums[q] + contracted_ref[j * steps + 8 * q : j * steps + 8 * q + 8, :] * factor
    side_ref[...] = fold(jnp.concatenate(sums, axis=0))


def times_inverse_kernel(own_ref, other_ref, space_gram_ref, inverse_ref, gram_ref):
    gram = unfold(own_ref[...] + other_ref[...])
    gram_ref[...] = gram
    inverse_ref[...] = ridge_inverse(gram * space_gram_ref[...])


def space_inverse_kernel(first_ref, second_ref, inverse_ref):
    inverse_ref[...] = ridge_inverse(first_ref[...] * second_ref[...])


def times_kernel(rows_ref, parts_ref, inverse_ref, params_ref, times_ref, gram_ref, side_ref, khatri_ref):
    steps, rank = times_ref.shape
    samples = params_ref.shape[0]
    times = dot(unfold(total(parts_ref)), inverse_ref[...], (1, 0), EXACT)
    times_ref[...] = times
    gram_ref[...] = gram_rows(times)
    for j in range(samples):
        factor = jnp.broadcast_to(params_ref[j : j + 1, :], times.shape)
        khatri_ref[j * steps : (j + 1) * steps, :] = (times * factor).astype(BF16)
    side_ref[...] = dot(khatri_ref[...], rows_ref[...], (0, 0))


HERE = pl.BlockSpec(memory_space=pltpu.VMEM)
AWAY = pl.BlockSpec(memory_space=pltpu.HBM)


def on_device(kernel, shapes, inputs, scratch=(), limit=8):
    return pl.pallas_call(
        kernel,
        out_shape=[s if isinstance(s, jax.ShapeDtypeStruct) else jax.ShapeDtypeStruct(s, F32) for s in shapes],
        in_specs=[HERE] * inputs if isinstance(inputs, int) else inputs,
        out_specs=[HERE] * len(shapes),
        scratch_shapes=list(scratch),
        compiler_params=pltpu.CompilerParams(vmem_limit_bytes=limit << 20),
    )


def exchange(copies, axes):
    return lax.all_to_all(copies, axes, split_axis=0, concat_axis=0, tiled=True)


def other_core(x):
    return lax.ppermute(x, CORE, [(0, 1), (1, 0)])


def per_device(snapshots, space_start, time_start):
    samples, steps, nodes = snapshots.shape
    rank = space_start.shape[0]
    plane, line = lax.axis_size(PLANE), lax.axis_size(LINE)
    width = 2 * rank
    both = (samples + rank) // 2
    count = samples * steps
    source = snapshots.reshape(count, nodes)
    times = time_start.T
    rows_shape = jax.ShapeDtypeStruct((count, nodes), BF16)
    start = on_device(
        start_kernel,
        [rows_shape, (count, rank), (plane, both, width)],
        [AWAY, AWAY, AWAY],
        [
            pltpu.VMEM((samples, rank), F32),
            pltpu.VMEM((rank, nodes), F32),
            pltpu.VMEM((steps, rank), F32),
            pltpu.SemaphoreType.DMA((samples // (GROUP * GROUPS),)),
            pltpu.SemaphoreType.DMA((2,)),
        ],
        24,
    )
    again = on_device(
        space_kernel, [(count, rank), (plane, both, width)], 5, [pltpu.VMEM((samples, rank), F32)], 24
    )
    last = on_device(last_kernel, [(rank, nodes)], 3)
    relay_both = on_device(relay_kernel, [(line, both, width)], 1)
    relay_times = on_device(relay_kernel, [(line, steps // 2, width)], 1)
    pair = on_device(pair_kernel, [(plane, steps // 2, width)], 2)
    for_params = on_device(params_kernel, [(samples, rank), (rank // 2, width), (rank, rank)], 2)
    time_side = on_device(time_side_kernel, [(steps // 2, width)], 2)
    times_inverse = on_device(times_inverse_kernel, [(rank, rank), (rank, rank)], 3)
    space_inverse = on_device(space_inverse_kernel, [(rank, rank)], 2)
    for_times = on_device(
        times_kernel, [(steps, rank), (rank, rank), (rank, nodes)], 4, [pltpu.VMEM((count, rank), BF16)], 24
    )
    away = [pltpu.with_memory_space_constraint(x, pltpu.HBM) for x in (source, space_start, times)]
    rows, contracted, message = start(*away)
    for sweep in range(SWEEPS):
        (message,) = relay_both(exchange(message, PLANE))
        params, gram, space_gram = for_params(exchange(message, LINE), times)
        other_gram = other_core(gram)
        (side,) = time_side(contracted, params)
        other_side = other_core(side)
        inverse, param_gram = times_inverse(gram, other_gram, space_gram)
        side, other_side, inverse = lax.optimization_barrier((side, other_side, inverse))
        (message,) = pair(side, other_side)
        (message,) = relay_times(exchange(message, PLANE))
        times, time_gram, side = for_times(rows, exchange(message, LINE), inverse, params)
        other = other_core(side)
        (inverse,) = space_inverse(param_gram, time_gram)
        if sweep + 1 < SWEEPS:
            contracted, message = again(rows, side, other, inverse, times)
        else:
            (space,) = last(side, other, inverse)
    return space, params.T, times.T


def solution(mesh):
    split = Mesh(
        mesh.devices.reshape(4, 8, 4, mesh.shape["params"]),
        ("nodes_0", "nodes_1", "nodes_2", "params"),
    )
    return jax.shard_map(
        per_device,
        mesh=split,
        in_specs=(P("params", None, NODES), P(None, NODES), P()),
        out_specs=(P(None, NODES), P(None, "params"), P()),
        check_vma=False,
    )
```

profile of v0, /device:TPU:1, one launch (start us, length us, event | category | flops | bytes accessed | tf_op | source)
XLA Modules:
  0.0 274.3 jit_solution(8590684061360482086)
XLA Ops:
  0.6 5.2 %shard_map.58 = (bf16[3072,1024]{1,0:T(8,128)(2,1)S(1)}, f32[3072,64]{1,0:T(8,128)S(1)}, f32[16,64,128]{2,1,0:T(8,128)S(1)}) custom-call(bf16[3072,1024]{1,0:T(8,128)(2,1)} %bitcast.7, f32[64,1024]{1,0:T(8,128)} %space_ref.1, f32[48,64]{1,0:T(8,128)} %bitcast.5), custom_call_target="tpu_custom_call" | custom-call | tf_op jit(solution)/shard_map/pallas_call | solution.py:271
  5.8 17.8 %all_to_all.80.parts_ref = f32[16,64,128]{2,1,0:T(8,128)S(1)} all-to-all(f32[16,64,128]{2,1,0:T(8,128)S(1)} %get-tuple-element.58), channel_id=1, replica_groups=mesh['nodes_0'=4,'nodes_1'=8,'nodes_2'=4,'params'=2] {'nodes_0','nodes_2'}, dimensions={0} | all-to-all | bytes 1048576 | tf_op jit(solution)/shard_map/all_to_all | solution.py:226
  23.6 17.4 %all_to_all.81.parts_ref = f32[8,64,128]{2,1,0:T(8,128)S(1)} all-to-all(f32[8,64,128]{2,1,0:T(8,128)S(1)} %shard_map.59), channel_id=1, replica_groups=mesh['nodes_0'=4,'nodes_1'=8,'nodes_2'=4,'params'=2] {'nodes_1'}, dimensions={0} | all-to-all | bytes 524288 | tf_op jit(solution)/shard_map/all_to_all | solution.py:226
  41.1 3.2 %shard_map.60 = (f32[64,64]{1,0:T(8,128)S(1)}, f32[32,128]{1,0:T(8,128)S(1)}, f32[64,64]{1,0:T(8,128)S(1)}) custom-call(f32[8,64,128]{2,1,0:T(8,128)S(1)} %all_to_all.81.parts_ref, f32[48,64]{1,0:T(8,128)S(1)} %bitcast.6), custom_call_target="tpu_custom_call" | custom-call | tf_op jit(solution)/shard_map/pallas_call | solution.py:274
  44.2 3.5 %collective-permute-start.1 = (f32[32,128]{1,0:T(8,128)S(1)}, f32[32,128]{1,0:T(8,128)S(1)}, u32[]{:S(2)}, u32[]{:S(2)}) collective-permute-start(f32[32,128]{1,0:T(8,128)S(1)} %get-tuple-element.60.own_ref), channel_id=1, source_target_pairs={{0,1},{1,0},{2,3},{3,2},{4,5},{5,4},{6,7},{7,6},{8,9},{9,8},{10,11... | collective-permute-start | bytes 49160 | tf_op jit(solution)/shard_map/ppermute | solution.py:230
  50.5 10.5 %all_to_all.82.parts_ref = f32[16,24,128]{2,1,0:T(8,128)S(1)} all-to-all(f32[16,24,128]{2,1,0:T(8,128)S(1)} %shard_map.63), channel_id=1, replica_groups=mesh['nodes_0'=4,'nodes_1'=8,'nodes_2'=4,'params'=2] {'nodes_0','nodes_2'}, dimensions={0} | all-to-all | bytes 393216 | tf_op jit(solution)/shard_map/all_to_all | solution.py:226
  61.0 10.0 %all_to_all.83.parts_ref = f32[8,24,128]{2,1,0:T(8,128)S(1)} all-to-all(f32[8,24,128]{2,1,0:T(8,128)S(1)} %shard_map.64), channel_id=1, replica_groups=mesh['nodes_0'=4,'nodes_1'=8,'nodes_2'=4,'params'=2] {'nodes_1'}, dimensions={0} | all-to-all | bytes 196608 | tf_op jit(solution)/shard_map/all_to_all | solution.py:226
  72.6 3.0 %collective-permute-start.2 = (f32[64,1024]{1,0:T(8,128)S(1)}, f32[64,1024]{1,0:T(8,128)S(1)}, u32[]{:S(2)}, u32[]{:S(2)}) collective-permute-start(f32[64,1024]{1,0:T(8,128)S(1)} %get-tuple-element.66.own_ref), channel_id=1, source_target_pairs={{0,1},{1,0},{2,3},{3,2},{4,5},{5,4},{6,7},{7,6},{8,9},{9,8},{10,11... | collective-permute-start | bytes 786440 | tf_op jit(solution)/shard_map/ppermute | solution.py:230
  77.4 3.2 %shard_map.67 = (f32[3072,64]{1,0:T(8,128)S(1)}, f32[16,64,128]{2,1,0:T(8,128)S(1)}) custom-call(bf16[3072,1024]{1,0:T(8,128)(2,1)S(1)} %get-tuple-element.56.rows_ref, f32[64,1024]{1,0:T(8,128)S(1)} %get-tuple-element.66.own_ref, f32[64,1024]{1,0:T(8,128)S(1)} %collective-permute-done.2.other_ref, f32[64,64]{1,0:T(8,128)S(1)} %shard_map.66.inverse_ref, ...), custom_call_target="tpu_custom_call" | custom-call | tf_op jit(solution)/shard_map/pallas_call | solution.py:286
  80.6 13.8 %all_to_all.84.parts_ref = f32[16,64,128]{2,1,0:T(8,128)S(1)} all-to-all(f32[16,64,128]{2,1,0:T(8,128)S(1)} %get-tuple-element.71), channel_id=1, replica_groups=mesh['nodes_0'=4,'nodes_1'=8,'nodes_2'=4,'params'=2] {'nodes_0','nodes_2'}, dimensions={0} | all-to-all | bytes 1048576 | tf_op jit(solution)/shard_map/all_to_all | solution.py:226
  94.4 12.6 %all_to_all.85.parts_ref = f32[8,64,128]{2,1,0:T(8,128)S(1)} all-to-all(f32[8,64,128]{2,1,0:T(8,128)S(1)} %shard_map.68), channel_id=1, replica_groups=mesh['nodes_0'=4,'nodes_1'=8,'nodes_2'=4,'params'=2] {'nodes_1'}, dimensions={0} | all-to-all | bytes 524288 | tf_op jit(solution)/shard_map/all_to_all | solution.py:226
  107.0 3.2 %shard_map.69 = (f32[64,64]{1,0:T(8,128)S(1)}, f32[32,128]{1,0:T(8,128)S(1)}, f32[64,64]{1,0:T(8,128)S(1)}) custom-call(f32[8,64,128]{2,1,0:T(8,128)S(1)} %all_to_all.85.parts_ref, f32[48,64]{1,0:T(8,128)S(1)} %get-tuple-element.69.times_ref), custom_call_target="tpu_custom_call" | custom-call | tf_op jit(solution)/shard_map/pallas_call | solution.py:274
  110.2 2.7 collective-permute-start.4
  115.7 10.3 %all_to_all.86.parts_ref = f32[16,24,128]{2,1,0:T(8,128)S(1)} all-to-all(f32[16,24,128]{2,1,0:T(8,128)S(1)} %shard_map.72), channel_id=1, replica_groups=mesh['nodes_0'=4,'nodes_1'=8,'nodes_2'=4,'params'=2] {'nodes_0','nodes_2'}, dimensions={0} | all-to-all | bytes 393216 | tf_op jit(solution)/shard_map/all_to_all | solution.py:226
  126.0 10.0 %all_to_all.87.parts_ref = f32[8,24,128]{2,1,0:T(8,128)S(1)} all-to-all(f32[8,24,128]{2,1,0:T(8,128)S(1)} %shard_map.73), channel_id=1, replica_groups=mesh['nodes_0'=4,'nodes_1'=8,'nodes_2'=4,'params'=2] {'nodes_1'}, dimensions={0} | all-to-all | bytes 196608 | tf_op jit(solution)/shard_map/all_to_all | solution.py:226
  137.5 3.0 %collective-permute-start.5 = (f32[64,1024]{1,0:T(8,128)S(1)}, f32[64,1024]{1,0:T(8,128)S(1)}, u32[]{:S(2)}, u32[]{:S(2)}) collective-permute-start(f32[64,1024]{1,0:T(8,128)S(1)} %get-tuple-element.79.own_ref), channel_id=1, source_target_pairs={{0,1},{1,0},{2,3},{3,2},{4,5},{5,4},{6,7},{7,6},{8,9},{9,8},{10,11... | collective-permute-start | bytes 786440 | tf_op jit(solution)/shard_map/ppermute | solution.py:230
  142.4 3.2 %shard_map.76 = (f32[3072,64]{1,0:T(8,128)S(1)}, f32[16,64,128]{2,1,0:T(8,128)S(1)}) custom-call(bf16[3072,1024]{1,0:T(8,128)(2,1)S(1)} %get-tuple-element.56.rows_ref, f32[64,1024]{1,0:T(8,128)S(1)} %get-tuple-element.79.own_ref, f32[64,1024]{1,0:T(8,128)S(1)} %collective-permute-done.5.other_ref, f32[64,64]{1,0:T(8,128)S(1)} %shard_map.75.inverse_ref, ...), custom_call_target="tpu_custom_call" | custom-call | tf_op jit(solution)/shard_map/pallas_call | solution.py:286
  145.6 13.8 %all_to_all.88.parts_ref = f32[16,64,128]{2,1,0:T(8,128)S(1)} all-to-all(f32[16,64,128]{2,1,0:T(8,128)S(1)} %get-tuple-element.84), channel_id=1, replica_groups=mesh['nodes_0'=4,'nodes_1'=8,'nodes_2'=4,'params'=2] {'nodes_0','nodes_2'}, dimensions={0} | all-to-all | bytes 1048576 | tf_op jit(solution)/shard_map/all_to_all | solution.py:226
  159.4 12.6 %all_to_all.89.parts_ref = f32[8,64,128]{2,1,0:T(8,128)S(1)} all-to-all(f32[8,64,128]{2,1,0:T(8,128)S(1)} %shard_map.77), channel_id=1, replica_groups=mesh['nodes_0'=4,'nodes_1'=8,'nodes_2'=4,'params'=2] {'nodes_1'}, dimensions={0} | all-to-all | bytes 524288 | tf_op jit(solution)/shard_map/all_to_all | solution.py:226
  172.0 3.2 %shard_map.78 = (f32[64,64]{1,0:T(8,128)S(1)}, f32[32,128]{1,0:T(8,128)S(1)}, f32[64,64]{1,0:T(8,128)S(1)}) custom-call(f32[8,64,128]{2,1,0:T(8,128)S(1)} %all_to_all.89.parts_ref, f32[48,64]{1,0:T(8,128)S(1)} %get-tuple-element.82.times_ref), custom_call_target="tpu_custom_call" | custom-call | tf_op jit(solution)/shard_map/pallas_call | solution.py:274
  175.2 2.7 collective-permute-start.7
  180.6 10.3 %all_to_all.90.parts_ref = f32[16,24,128]{2,1,0:T(8,128)S(1)} all-to-all(f32[16,24,128]{2,1,0:T(8,128)S(1)} %shard_map.81), channel_id=1, replica_groups=mesh['nodes_0'=4,'nodes_1'=8,'nodes_2'=4,'params'=2] {'nodes_0','nodes_2'}, dimensions={0} | all-to-all | bytes 393216 | tf_op jit(solution)/shard_map/all_to_all | solution.py:226
  190.9 10.0 %all_to_all.91.parts_ref = f32[8,24,128]{2,1,0:T(8,128)S(1)} all-to-all(f32[8,24,128]{2,1,0:T(8,128)S(1)} %shard_map.82), channel_id=1, replica_groups=mesh['nodes_0'=4,'nodes_1'=8,'nodes_2'=4,'params'=2] {'nodes_1'}, dimensions={0} | all-to-all | bytes 196608 | tf_op jit(solution)/shard_map/all_to_all | solution.py:226
  202.5 3.2 %collective-permute-start.8 = (f32[64,1024]{1,0:T(8,128)S(1)}, f32[64,1024]{1,0:T(8,128)S(1)}, u32[]{:S(2)}, u32[]{:S(2)}) collective-permute-start(f32[64,1024]{1,0:T(8,128)S(1)} %get-tuple-element.92.own_ref), channel_id=1, source_target_pairs={{0,1},{1,0},{2,3},{3,2},{4,5},{5,4},{6,7},{7,6},{8,9},{9,8},{10,11... | collective-permute-start | bytes 786440 | tf_op jit(solution)/shard_map/ppermute | solution.py:230
  207.6 3.2 %shard_map.85 = (f32[3072,64]{1,0:T(8,128)S(1)}, f32[16,64,128]{2,1,0:T(8,128)S(1)}) custom-call(bf16[3072,1024]{1,0:T(8,128)(2,1)S(1)} %get-tuple-element.56.rows_ref, f32[64,1024]{1,0:T(8,128)S(1)} %get-tuple-element.92.own_ref, f32[64,1024]{1,0:T(8,128)S(1)} %collective-permute-done.8.other_ref, f32[64,64]{1,0:T(8,128)S(1)} %shard_map.84.inverse_ref, ...), custom_call_target="tpu_custom_call" | custom-call | tf_op jit(solution)/shard_map/pallas_call | solution.py:286
  210.7 13.8 %all_to_all.92.parts_ref = f32[16,64,128]{2,1,0:T(8,128)S(1)} all-to-all(f32[16,64,128]{2,1,0:T(8,128)S(1)} %get-tuple-element.97), channel_id=1, replica_groups=mesh['nodes_0'=4,'nodes_1'=8,'nodes_2'=4,'params'=2] {'nodes_0','nodes_2'}, dimensions={0} | all-to-all | bytes 1048576 | tf_op jit(solution)/shard_map/all_to_all | solution.py:226
  224.5 12.6 %all_to_all.93.parts_ref = f32[8,64,128]{2,1,0:T(8,128)S(1)} all-to-all(f32[8,64,128]{2,1,0:T(8,128)S(1)} %shard_map.86), channel_id=1, replica_groups=mesh['nodes_0'=4,'nodes_1'=8,'nodes_2'=4,'params'=2] {'nodes_1'}, dimensions={0} | all-to-all | bytes 524288 | tf_op jit(solution)/shard_map/all_to_all | solution.py:226
  237.2 3.2 %shard_map.87 = (f32[64,64]{1,0:T(8,128)S(1)}, f32[32,128]{1,0:T(8,128)S(1)}, f32[64,64]{1,0:T(8,128)S(1)}) custom-call(f32[8,64,128]{2,1,0:T(8,128)S(1)} %all_to_all.93.parts_ref, f32[48,64]{1,0:T(8,128)S(1)} %get-tuple-element.95.times_ref), custom_call_target="tpu_custom_call" | custom-call | tf_op jit(solution)/shard_map/pallas_call | solution.py:274
  240.3 2.7 collective-permute-start.10
  245.8 10.3 %all_to_all.94.parts_ref = f32[16,24,128]{2,1,0:T(8,128)S(1)} all-to-all(f32[16,24,128]{2,1,0:T(8,128)S(1)} %shard_map.90), channel_id=1, replica_groups=mesh['nodes_0'=4,'nodes_1'=8,'nodes_2'=4,'params'=2] {'nodes_0','nodes_2'}, dimensions={0} | all-to-all | bytes 393216 | tf_op jit(solution)/shard_map/all_to_all | solution.py:226
  256.1 10.0 %all_to_all.95.parts_ref = f32[8,24,128]{2,1,0:T(8,128)S(1)} all-to-all(f32[8,24,128]{2,1,0:T(8,128)S(1)} %shard_map.91), channel_id=1, replica_groups=mesh['nodes_0'=4,'nodes_1'=8,'nodes_2'=4,'params'=2] {'nodes_1'}, dimensions={0} | all-to-all | bytes 196608 | tf_op jit(solution)/shard_map/all_to_all | solution.py:226
  267.7 3.0 %collective-permute-start.11 = (f32[64,1024]{1,0:T(8,128)S(1)}, f32[64,1024]{1,0:T(8,128)S(1)}, u32[]{:S(2)}, u32[]{:S(2)}) collective-permute-start(f32[64,1024]{1,0:T(8,128)S(1)} %get-tuple-element.105.own_ref), channel_id=1, source_target_pairs={{0,1},{1,0},{2,3},{3,2},{4,5},{5,4},{6,7},{7,6},{8,9},{9,8},{10,11... | collective-permute-start | bytes 786440 | tf_op jit(solution)/shard_map/ppermute | solution.py:230
  (48 shorter events, 26.9 us)
Async XLA Ops:
  5.8 35.3 %copy-start = (f32[64,48]{0,1:T(8,128)S(1)}, f32[64,48]{0,1:T(8,128)}, u32[]{:S(2)}) copy-start(f32[64,48]{0,1:T(8,128)} %param.5) | copy-start | bytes 36868
  44.2 4.3 %collective-permute-start.1 = (f32[32,128]{1,0:T(8,128)S(1)}, f32[32,128]{1,0:T(8,128)S(1)}, u32[]{:S(2)}, u32[]{:S(2)}) collective-permute-start(f32[32,128]{1,0:T(8,128)S(1)} %get-tuple-element.60.own_ref), channel_id=1, source_target_pairs={{0,1},{1,0},{2,3},{3,2},{4,5},{5,4},{6,7},{7,6},{8,9},{9,8},{10,11... | collective-permute-start | bytes 49160 | tf_op jit(solution)/shard_map/ppermute | solution.py:230
  47.9 2.6 collective-permute-start
  72.6 4.8 %collective-permute-start.2 = (f32[64,1024]{1,0:T(8,128)S(1)}, f32[64,1024]{1,0:T(8,128)S(1)}, u32[]{:S(2)}, u32[]{:S(2)}) collective-permute-start(f32[64,1024]{1,0:T(8,128)S(1)} %get-tuple-element.66.own_ref), channel_id=1, source_target_pairs={{0,1},{1,0},{2,3},{3,2},{4,5},{5,4},{6,7},{7,6},{8,9},{9,8},{10,11... | collective-permute-start | bytes 786440 | tf_op jit(solution)/shard_map/ppermute | solution.py:230
  110.2 3.5 %collective-permute-start.4 = (f32[32,128]{1,0:T(8,128)S(1)}, f32[32,128]{1,0:T(8,128)S(1)}, u32[]{:S(2)}, u32[]{:S(2)}) collective-permute-start(f32[32,128]{1,0:T(8,128)S(1)} %get-tuple-element.73.own_ref), channel_id=1, source_target_pairs={{0,1},{1,0},{2,3},{3,2},{4,5},{5,4},{6,7},{7,6},{8,9},{9,8},{10,11... | collective-permute-start | bytes 49160 | tf_op jit(solution)/shard_map/ppermute | solution.py:230
  113.1 2.6 collective-permute-start.3
  137.5 4.9 %collective-permute-start.5 = (f32[64,1024]{1,0:T(8,128)S(1)}, f32[64,1024]{1,0:T(8,128)S(1)}, u32[]{:S(2)}, u32[]{:S(2)}) collective-permute-start(f32[64,1024]{1,0:T(8,128)S(1)} %get-tuple-element.79.own_ref), channel_id=1, source_target_pairs={{0,1},{1,0},{2,3},{3,2},{4,5},{5,4},{6,7},{7,6},{8,9},{9,8},{10,11... | collective-permute-start | bytes 786440 | tf_op jit(solution)/shard_map/ppermute | solution.py:230
  175.2 3.5 %collective-permute-start.7 = (f32[32,128]{1,0:T(8,128)S(1)}, f32[32,128]{1,0:T(8,128)S(1)}, u32[]{:S(2)}, u32[]{:S(2)}) collective-permute-start(f32[32,128]{1,0:T(8,128)S(1)} %get-tuple-element.86.own_ref), channel_id=1, source_target_pairs={{0,1},{1,0},{2,3},{3,2},{4,5},{5,4},{6,7},{7,6},{8,9},{9,8},{10,11... | collective-permute-start | bytes 49160 | tf_op jit(solution)/shard_map/ppermute | solution.py:230
  178.0 2.6 collective-permute-start.6
  202.5 5.1 %collective-permute-start.8 = (f32[64,1024]{1,0:T(8,128)S(1)}, f32[64,1024]{1,0:T(8,128)S(1)}, u32[]{:S(2)}, u32[]{:S(2)}) collective-permute-start(f32[64,1024]{1,0:T(8,128)S(1)} %get-tuple-element.92.own_ref), channel_id=1, source_target_pairs={{0,1},{1,0},{2,3},{3,2},{4,5},{5,4},{6,7},{7,6},{8,9},{9,8},{10,11... | collective-permute-start | bytes 786440 | tf_op jit(solution)/shard_map/ppermute | solution.py:230
  240.3 3.5 %collective-permute-start.10 = (f32[32,128]{1,0:T(8,128)S(1)}, f32[32,128]{1,0:T(8,128)S(1)}, u32[]{:S(2)}, u32[]{:S(2)}) collective-permute-start(f32[32,128]{1,0:T(8,128)S(1)} %get-tuple-element.99.own_ref), channel_id=1, source_target_pairs={{0,1},{1,0},{2,3},{3,2},{4,5},{5,4},{6,7},{7,6},{8,9},{9,8},{10,11... | collective-permute-start | bytes 49160 | tf_op jit(solution)/shard_map/ppermute | solution.py:230
  243.2 2.6 collective-permute-start.9
  267.7 5.5 %collective-permute-start.11 = (f32[64,1024]{1,0:T(8,128)S(1)}, f32[64,1024]{1,0:T(8,128)S(1)}, u32[]{:S(2)}, u32[]{:S(2)}) collective-permute-start(f32[64,1024]{1,0:T(8,128)S(1)} %get-tuple-element.105.own_ref), channel_id=1, source_target_pairs={{0,1},{1,0},{2,3},{3,2},{4,5},{5,4},{6,7},{7,6},{8,9},{9,8},{10,11... | collective-permute-start | bytes 786440 | tf_op jit(solution)/shard_map/ppermute | solution.py:230
where the time goes:
time: 275 us; the launch traced here: 274 us
  blocking collectives  196 us (71%)
  Pallas kernels  51 us (19%)
  starting transfers between devices  24.1 us (9%)
    all_to_all x16, blocking collectives, exchange(): return lax.all_to_all(copies, axes, split_axis=0, concat_axis=0, tiled=True)  196 us
    ppermute x12, starting transfers between devices, other_core(): return lax.ppermute(x, CORE, [(0, 1), (1, 0)])  24.1 us
    pallas_call x4, Pallas kernels, per_device(): params, gram, space_gram = for_params(exchange(message, LINE), times)  12.6 us
    pallas_call x3, Pallas kernels, per_device(): contracted, message = again(rows, side, other, inverse, times)  9.55 us
    pallas_call x4, Pallas kernels, per_device(): inverse, param_gram = times_inverse(gram, other_gram, space_gram)  7.71 us
    pallas_call x4, Pallas kernels, per_device(): inverse, = space_inverse(param_gram, time_gram)  7.53 us
    pallas_call x4, Pallas kernels, per_device(): for_times(rows, exchange(message, LINE), inverse, params)  6.24 us
  transfers between devices with their start and end apart: 12, of which 4 were waited for; matrix products, arithmetic and copies ran while one was open for 0% of the time, Pallas kernels for 6%

commit v1 on v0

--- a/solution.py
+++ b/solution.py
@@ -85,6 +85,32 @@
     return jnp.concatenate([x[:, :half], x[:, half:]], axis=0)
 
 
+def pack(gram):
+    half = gram.shape[0] // 2
+    row = lax.broadcasted_iota(jnp.int32, (half, half), 0)
+    column = lax.broadcasted_iota(jnp.int32, (half, half), 1)
+    first, cross, last = gram[:half, :half], gram[:half, half:], gram[half:, half:]
+    body = fold(jnp.concatenate([jnp.where(row <= column, first, last), cross], axis=1))
+    diagonal = jnp.sum(jnp.where(row == column, last, 0.0), axis=0, keepdims=True)
+    blank = jnp.zeros((1, body.shape[1] - half), F32)
+    return body, jnp.concatenate([diagonal, blank], axis=1)
+
+
+def unpack(body, tail):
+    body = unfold(body)
+    half = body.shape[0]
+    row = lax.broadcasted_iota(jnp.int32, (half, half), 0)
+    column = lax.broadcasted_iota(jnp.int32, (half, half), 1)
+    mixed, cross = body[:, :half], body[:, half:]
+    turned = mixed.T
+    first = jnp.where(row <= column, mixed, turned)
+    diagonal = jnp.broadcast_to(tail[:, :half], (half, half))
+    last = jnp.where(row > column, mixed, jnp.where(row < column, turned, diagonal))
+    return jnp.concatenate(
+        [jnp.concatenate([first, cross], axis=1), jnp.concatenate([cross.T, last], axis=1)], axis=0
+    )
+
+
 def total(parts):
     whole = [parts[i] for i in range(parts.shape[0])]
     while len(whole) > 1:
@@ -101,7 +127,10 @@
     steps, rank = times.shape
     samples = side_ref.shape[0]
     low = space.astype(BF16)
-    spread(message_ref, fold(dot(space, space, (1, 1), EXACT)), slice(samples // 2, None))
+    body, tail = pack(dot(space, space, (1, 1), EXACT))
+    split = samples // 2 + rank // 4
+    spread(message_ref, body, slice(samples // 2, split))
+    spread(message_ref, tail, slice(split, split + 1))
 
     def groups(step, carry):
         if arrive is not None:
@@ -122,7 +151,18 @@
 
 
 def start_kernel(
-    source_ref, space_ref, times_ref, rows_ref, contracted_ref, message_ref, side_ref, space_here, times_here, arrived, early
+    source_ref,
+    space_ref,
+    times_ref,
+    rows_ref,
+    contracted_ref,
+    message_ref,
+    gram_ref,
+    side_ref,
+    space_here,
+    times_here,
+    arrived,
+    early,
 ):
     count = arrived.shape[0]
     size = rows_ref.shape[0] // count
@@ -141,6 +181,7 @@
         load(i).start()
     for copy in others:
         copy.wait()
+    gram_ref[...] = gram_rows(times_here[...])
     contract(
         rows_ref, space_here[...], times_here[...], contracted_ref, message_ref, side_ref, lambda step: load(step).wait()
     )
@@ -163,12 +204,13 @@
     spread(copies_ref, own_ref[...] + other_ref[...])
 
 
-def params_kernel(parts_ref, times_ref, params_ref, gram_ref, space_gram_ref):
+def params_kernel(parts_ref, time_gram_ref, params_ref, gram_ref, space_gram_ref):
     half = params_ref.shape[0] // 2
     whole = total(parts_ref)
-    side, space_gram = unfold(whole[:half, :]), unfold(whole[half:, :])
+    split = whole.shape[0] - 1
+    side, space_gram = unfold(whole[:half, :]), unpack(whole[half:split, :], whole[split:, :])
     space_gram_ref[...] = space_gram
-    inverse = ridge_inverse(space_gram * gram_rows(times_ref[...]))
+    inverse = ridge_inverse(space_gram * time_gram_ref[...])
     params = dot(side, inverse, (1, 0), EXACT)
     params_ref[...] = params
     gram_ref[...] = fold(gram_rows(params))
@@ -235,14 +277,14 @@
     rank = space_start.shape[0]
     plane, line = lax.axis_size(PLANE), lax.axis_size(LINE)
     width = 2 * rank
-    both = (samples + rank) // 2
+    both = samples // 2 + rank // 4 + 1
     count = samples * steps
     source = snapshots.reshape(count, nodes)
     times = time_start.T
     rows_shape = jax.ShapeDtypeStruct((count, nodes), BF16)
     start = on_device(
         start_kernel,
-        [rows_shape, (count, rank), (plane, both, width)],
+        [rows_shape, (count, rank), (plane, both, width), (rank, rank)],
         [AWAY, AWAY, AWAY],
         [
             pltpu.VMEM((samples, rank), F32),
@@ -268,10 +310,10 @@
         times_kernel, [(steps, rank), (rank, rank), (rank, nodes)], 4, [pltpu.VMEM((count, rank), BF16)], 24
     )
     away = [pltpu.with_memory_space_constraint(x, pltpu.HBM) for x in (source, space_start, times)]
-    rows, contracted, message = start(*away)
+    rows, contracted, message, time_gram = start(*away)
     for sweep in range(SWEEPS):
         (message,) = relay_both(exchange(message, PLANE))
-        params, gram, space_gram = for_params(exchange(message, LINE), times)
+        params, gram, space_gram = for_params(exchange(message, LINE), time_gram)
         other_gram = other_core(gram)
         (side,) = time_side(contracted, params)
         other_side = other_core(side)

time: 275 us -> 269 us (0.978)
  blocking collectives: 196 us -> 190 us
    all_to_all x16, blocking collectives: 196 us -> 190 us  [exchange(): return lax.all_to_all(copies, axes, split_axis=0, concat_axis=0, tiled=True)]
where the time goes in v1:
time: 269 us
  blocking collectives  190 us (71%)
  Pallas kernels  51.2 us (19%)
  starting transfers between devices  24.2 us (9%)
    all_to_all x16, blocking collectives, exchange(): return lax.all_to_all(copies, axes, split_axis=0, concat_axis=0, tiled=True)  190 us
    ppermute x12, starting transfers between devices, other_core(): return lax.ppermute(x, CORE, [(0, 1), (1, 0)])  24.2 us
    pallas_call x4, Pallas kernels, per_device(): params, gram, space_gram = for_params(exchange(message, LINE), time_gram)  12.7 us
    pallas_call x3, Pallas kernels, per_device(): contracted, message = again(rows, side, other, inverse, times)  9.69 us
    pallas_call x4, Pallas kernels, per_device(): inverse, param_gram = times_inverse(gram, other_gram, space_gram)  7.7 us
    pallas_call x4, Pallas kernels, per_device(): inverse, = space_inverse(param_gram, time_gram)  7.53 us
    pallas_call x4, Pallas kernels, per_device(): for_times(rows, exchange(message, LINE), inverse, params)  6.24 us
  transfers between devices with their start and end apart: 12, of which 4 were waited for; matrix products, arithmetic and copies ran while one was open for 0% of the time, Pallas kernels for 6%

profile of v1, /device:TPU:1, one launch (start us, length us, event | category | flops | bytes accessed | tf_op | source)
XLA Modules:
  0.0 268.6 jit_solution(6813994888771928719)
XLA Ops:
  0.6 5.3 %shard_map.58 = (bf16[3072,1024]{1,0:T(8,128)(2,1)S(1)}, f32[3072,64]{1,0:T(8,128)S(1)}, f32[16,49,128]{2,1,0:T(8,128)S(1)}, f32[64,64]{1,0:T(8,128)S(1)}) custom-call(bf16[3072,1024]{1,0:T(8,128)(2,1)} %bitcast.5, f32[64,1024]{1,0:T(8,128)} %space_ref.1, f32[48,64]{1,0:T(8,128)} %bitcast.6), custom_call_target="tpu_custom_call" | custom-call | tf_op jit(solution)/shard_map/pallas_call | solution.py:313
  5.9 17.3 %all_to_all.80.parts_ref = f32[16,49,128]{2,1,0:T(8,128)S(1)} all-to-all(f32[16,49,128]{2,1,0:T(8,128)S(1)} %get-tuple-element.59), channel_id=1, replica_groups=mesh['nodes_0'=4,'nodes_1'=8,'nodes_2'=4,'params'=2] {'nodes_0','nodes_2'}, dimensions={0} | all-to-all | bytes 802816 | tf_op jit(solution)/shard_map/all_to_all | solution.py:268
  23.2 17.1 %all_to_all.81.parts_ref = f32[8,49,128]{2,1,0:T(8,128)S(1)} all-to-all(f32[8,49,128]{2,1,0:T(8,128)S(1)} %shard_map.59), channel_id=1, replica_groups=mesh['nodes_0'=4,'nodes_1'=8,'nodes_2'=4,'params'=2] {'nodes_1'}, dimensions={0} | all-to-all | bytes 401408 | tf_op jit(solution)/shard_map/all_to_all | solution.py:268
  40.3 3.2 %shard_map.60 = (f32[64,64]{1,0:T(8,128)S(1)}, f32[32,128]{1,0:T(8,128)S(1)}, f32[64,64]{1,0:T(8,128)S(1)}) custom-call(f32[8,49,128]{2,1,0:T(8,128)S(1)} %all_to_all.81.parts_ref, f32[64,64]{1,0:T(8,128)S(1)} %get-tuple-element.60.time_gram_ref), custom_call_target="tpu_custom_call" | custom-call | tf_op jit(solution)/shard_map/pallas_call | solution.py:316
  43.5 3.2 %collective-permute-start.1 = (f32[32,128]{1,0:T(8,128)S(1)}, f32[32,128]{1,0:T(8,128)S(1)}, u32[]{:S(2)}, u32[]{:S(2)}) collective-permute-start(f32[32,128]{1,0:T(8,128)S(1)} %get-tuple-element.62.own_ref), channel_id=1, source_target_pairs={{0,1},{1,0},{2,3},{3,2},{4,5},{5,4},{6,7},{7,6},{8,9},{9,8},{10,11... | collective-permute-start | bytes 49160 | tf_op jit(solution)/shard_map/ppermute | solution.py:272
  49.5 10.1 %all_to_all.82.parts_ref = f32[16,24,128]{2,1,0:T(8,128)S(1)} all-to-all(f32[16,24,128]{2,1,0:T(8,128)S(1)} %shard_map.63), channel_id=1, replica_groups=mesh['nodes_0'=4,'nodes_1'=8,'nodes_2'=4,'params'=2] {'nodes_0','nodes_2'}, dimensions={0} | all-to-all | bytes 393216 | tf_op jit(solution)/shard_map/all_to_all | solution.py:268
  59.6 10.0 %all_to_all.83.parts_ref = f32[8,24,128]{2,1,0:T(8,128)S(1)} all-to-all(f32[8,24,128]{2,1,0:T(8,128)S(1)} %shard_map.64), channel_id=1, replica_groups=mesh['nodes_0'=4,'nodes_1'=8,'nodes_2'=4,'params'=2] {'nodes_1'}, dimensions={0} | all-to-all | bytes 196608 | tf_op jit(solution)/shard_map/all_to_all | solution.py:268
  71.2 3.0 %collective-permute-start.2 = (f32[64,1024]{1,0:T(8,128)S(1)}, f32[64,1024]{1,0:T(8,128)S(1)}, u32[]{:S(2)}, u32[]{:S(2)}) collective-permute-start(f32[64,1024]{1,0:T(8,128)S(1)} %get-tuple-element.68.own_ref), channel_id=1, source_target_pairs={{0,1},{1,0},{2,3},{3,2},{4,5},{5,4},{6,7},{7,6},{8,9},{9,8},{10,11... | collective-permute-start | bytes 786440 | tf_op jit(solution)/shard_map/ppermute | solution.py:272
  76.0 3.2 %shard_map.67 = (f32[3072,64]{1,0:T(8,128)S(1)}, f32[16,49,128]{2,1,0:T(8,128)S(1)}) custom-call(bf16[3072,1024]{1,0:T(8,128)(2,1)S(1)} %get-tuple-element.57.rows_ref, f32[64,1024]{1,0:T(8,128)S(1)} %get-tuple-element.68.own_ref, f32[64,1024]{1,0:T(8,128)S(1)} %collective-permute-done.2.other_ref, f32[64,64]{1,0:T(8,128)S(1)} %shard_map.66.inverse_ref, ...), custom_call_target="tpu_custom_call" | custom-call | tf_op jit(solution)/shard_map/pallas_call | solution.py:328
  79.3 13.0 %all_to_all.84.parts_ref = f32[16,49,128]{2,1,0:T(8,128)S(1)} all-to-all(f32[16,49,128]{2,1,0:T(8,128)S(1)} %get-tuple-element.73), channel_id=1, replica_groups=mesh['nodes_0'=4,'nodes_1'=8,'nodes_2'=4,'params'=2] {'nodes_0','nodes_2'}, dimensions={0} | all-to-all | bytes 802816 | tf_op jit(solution)/shard_map/all_to_all | solution.py:268
  92.3 11.8 %all_to_all.85.parts_ref = f32[8,49,128]{2,1,0:T(8,128)S(1)} all-to-all(f32[8,49,128]{2,1,0:T(8,128)S(1)} %shard_map.68), channel_id=1, replica_groups=mesh['nodes_0'=4,'nodes_1'=8,'nodes_2'=4,'params'=2] {'nodes_1'}, dimensions={0} | all-to-all | bytes 401408 | tf_op jit(solution)/shard_map/all_to_all | solution.py:268
  104.1 3.2 %shard_map.69 = (f32[64,64]{1,0:T(8,128)S(1)}, f32[32,128]{1,0:T(8,128)S(1)}, f32[64,64]{1,0:T(8,128)S(1)}) custom-call(f32[8,49,128]{2,1,0:T(8,128)S(1)} %all_to_all.85.parts_ref, f32[64,64]{1,0:T(8,128)S(1)} %get-tuple-element.70.second_ref.time_gram_ref), custom_call_target="tpu_custom_call" | custom-call | tf_op jit(solution)/shard_map/pallas_call | solution.py:316
  107.3 2.8 %collective-permute-start.4 = (f32[32,128]{1,0:T(8,128)S(1)}, f32[32,128]{1,0:T(8,128)S(1)}, u32[]{:S(2)}, u32[]{:S(2)}) collective-permute-start(f32[32,128]{1,0:T(8,128)S(1)} %get-tuple-element.75.own_ref), channel_id=1, source_target_pairs={{0,1},{1,0},{2,3},{3,2},{4,5},{5,4},{6,7},{7,6},{8,9},{9,8},{10,11... | collective-permute-start | bytes 49160 | tf_op jit(solution)/shard_map/ppermute | solution.py:272
  112.9 10.2 %all_to_all.86.parts_ref = f32[16,24,128]{2,1,0:T(8,128)S(1)} all-to-all(f32[16,24,128]{2,1,0:T(8,128)S(1)} %shard_map.72), channel_id=1, replica_groups=mesh['nodes_0'=4,'nodes_1'=8,'nodes_2'=4,'params'=2] {'nodes_0','nodes_2'}, dimensions={0} | all-to-all | bytes 393216 | tf_op jit(solution)/shard_map/all_to_all | solution.py:268
  123.1 10.0 %all_to_all.87.parts_ref = f32[8,24,128]{2,1,0:T(8,128)S(1)} all-to-all(f32[8,24,128]{2,1,0:T(8,128)S(1)} %shard_map.73), channel_id=1, replica_groups=mesh['nodes_0'=4,'nodes_1'=8,'nodes_2'=4,'params'=2] {'nodes_1'}, dimensions={0} | all-to-all | bytes 196608 | tf_op jit(solution)/shard_map/all_to_all | solution.py:268
  134.7 3.0 %collective-permute-start.5 = (f32[64,1024]{1,0:T(8,128)S(1)}, f32[64,1024]{1,0:T(8,128)S(1)}, u32[]{:S(2)}, u32[]{:S(2)}) collective-permute-start(f32[64,1024]{1,0:T(8,128)S(1)} %get-tuple-element.81.own_ref), channel_id=1, source_target_pairs={{0,1},{1,0},{2,3},{3,2},{4,5},{5,4},{6,7},{7,6},{8,9},{9,8},{10,11... | collective-permute-start | bytes 786440 | tf_op jit(solution)/shard_map/ppermute | solution.py:272
  139.6 3.2 %shard_map.76 = (f32[3072,64]{1,0:T(8,128)S(1)}, f32[16,49,128]{2,1,0:T(8,128)S(1)}) custom-call(bf16[3072,1024]{1,0:T(8,128)(2,1)S(1)} %get-tuple-element.57.rows_ref, f32[64,1024]{1,0:T(8,128)S(1)} %get-tuple-element.81.own_ref, f32[64,1024]{1,0:T(8,128)S(1)} %collective-permute-done.5.other_ref, f32[64,64]{1,0:T(8,128)S(1)} %shard_map.75.inverse_ref, ...), custom_call_target="tpu_custom_call" | custom-call | tf_op jit(solution)/shard_map/pallas_call | solution.py:328
  142.8 13.0 %all_to_all.88.parts_ref = f32[16,49,128]{2,1,0:T(8,128)S(1)} all-to-all(f32[16,49,128]{2,1,0:T(8,128)S(1)} %get-tuple-element.86), channel_id=1, replica_groups=mesh['nodes_0'=4,'nodes_1'=8,'nodes_2'=4,'params'=2] {'nodes_0','nodes_2'}, dimensions={0} | all-to-all | bytes 802816 | tf_op jit(solution)/shard_map/all_to_all | solution.py:268
  155.9 11.8 %all_to_all.89.parts_ref = f32[8,49,128]{2,1,0:T(8,128)S(1)} all-to-all(f32[8,49,128]{2,1,0:T(8,128)S(1)} %shard_map.77), channel_id=1, replica_groups=mesh['nodes_0'=4,'nodes_1'=8,'nodes_2'=4,'params'=2] {'nodes_1'}, dimensions={0} | all-to-all | bytes 401408 | tf_op jit(solution)/shard_map/all_to_all | solution.py:268
  167.6 3.2 %shard_map.78 = (f32[64,64]{1,0:T(8,128)S(1)}, f32[32,128]{1,0:T(8,128)S(1)}, f32[64,64]{1,0:T(8,128)S(1)}) custom-call(f32[8,49,128]{2,1,0:T(8,128)S(1)} %all_to_all.89.parts_ref, f32[64,64]{1,0:T(8,128)S(1)} %get-tuple-element.83.second_ref.time_gram_ref), custom_call_target="tpu_custom_call" | custom-call | tf_op jit(solution)/shard_map/pallas_call | solution.py:316
  170.8 2.9 %collective-permute-start.7 = (f32[32,128]{1,0:T(8,128)S(1)}, f32[32,128]{1,0:T(8,128)S(1)}, u32[]{:S(2)}, u32[]{:S(2)}) collective-permute-start(f32[32,128]{1,0:T(8,128)S(1)} %get-tuple-element.88.own_ref), channel_id=1, source_target_pairs={{0,1},{1,0},{2,3},{3,2},{4,5},{5,4},{6,7},{7,6},{8,9},{9,8},{10,11... | collective-permute-start | bytes 49160 | tf_op jit(solution)/shard_map/ppermute | solution.py:272
  176.4 10.2 %all_to_all.90.parts_ref = f32[16,24,128]{2,1,0:T(8,128)S(1)} all-to-all(f32[16,24,128]{2,1,0:T(8,128)S(1)} %shard_map.81), channel_id=1, replica_groups=mesh['nodes_0'=4,'nodes_1'=8,'nodes_2'=4,'params'=2] {'nodes_0','nodes_2'}, dimensions={0} | all-to-all | bytes 393216 | tf_op jit(solution)/shard_map/all_to_all | solution.py:268
  186.7 10.0 %all_to_all.91.parts_ref = f32[8,24,128]{2,1,0:T(8,128)S(1)} all-to-all(f32[8,24,128]{2,1,0:T(8,128)S(1)} %shard_map.82), channel_id=1, replica_groups=mesh['nodes_0'=4,'nodes_1'=8,'nodes_2'=4,'params'=2] {'nodes_1'}, dimensions={0} | all-to-all | bytes 196608 | tf_op jit(solution)/shard_map/all_to_all | solution.py:268
  198.2 3.2 %collective-permute-start.8 = (f32[64,1024]{1,0:T(8,128)S(1)}, f32[64,1024]{1,0:T(8,128)S(1)}, u32[]{:S(2)}, u32[]{:S(2)}) collective-permute-start(f32[64,1024]{1,0:T(8,128)S(1)} %get-tuple-element.94.own_ref), channel_id=1, source_target_pairs={{0,1},{1,0},{2,3},{3,2},{4,5},{5,4},{6,7},{7,6},{8,9},{9,8},{10,11... | collective-permute-start | bytes 786440 | tf_op jit(solution)/shard_map/ppermute | solution.py:272
  203.3 3.2 %shard_map.85 = (f32[3072,64]{1,0:T(8,128)S(1)}, f32[16,49,128]{2,1,0:T(8,128)S(1)}) custom-call(bf16[3072,1024]{1,0:T(8,128)(2,1)S(1)} %get-tuple-element.57.rows_ref, f32[64,1024]{1,0:T(8,128)S(1)} %get-tuple-element.94.own_ref, f32[64,1024]{1,0:T(8,128)S(1)} %collective-permute-done.8.other_ref, f32[64,64]{1,0:T(8,128)S(1)} %shard_map.84.inverse_ref, ...), custom_call_target="tpu_custom_call" | custom-call | tf_op jit(solution)/shard_map/pallas_call | solution.py:328
  206.5 13.0 %all_to_all.92.parts_ref = f32[16,49,128]{2,1,0:T(8,128)S(1)} all-to-all(f32[16,49,128]{2,1,0:T(8,128)S(1)} %get-tuple-element.99), channel_id=1, replica_groups=mesh['nodes_0'=4,'nodes_1'=8,'nodes_2'=4,'params'=2] {'nodes_0','nodes_2'}, dimensions={0} | all-to-all | bytes 802816 | tf_op jit(solution)/shard_map/all_to_all | solution.py:268
  219.6 11.8 %all_to_all.93.parts_ref = f32[8,49,128]{2,1,0:T(8,128)S(1)} all-to-all(f32[8,49,128]{2,1,0:T(8,128)S(1)} %shard_map.86), channel_id=1, replica_groups=mesh['nodes_0'=4,'nodes_1'=8,'nodes_2'=4,'params'=2] {'nodes_1'}, dimensions={0} | all-to-all | bytes 401408 | tf_op jit(solution)/shard_map/all_to_all | solution.py:268
  231.4 3.2 %shard_map.87 = (f32[64,64]{1,0:T(8,128)S(1)}, f32[32,128]{1,0:T(8,128)S(1)}, f32[64,64]{1,0:T(8,128)S(1)}) custom-call(f32[8,49,128]{2,1,0:T(8,128)S(1)} %all_to_all.93.parts_ref, f32[64,64]{1,0:T(8,128)S(1)} %get-tuple-element.96.second_ref.time_gram_ref), custom_call_target="tpu_custom_call" | custom-call | tf_op jit(solution)/shard_map/pallas_call | solution.py:316
  234.6 2.8 %collective-permute-start.10 = (f32[32,128]{1,0:T(8,128)S(1)}, f32[32,128]{1,0:T(8,128)S(1)}, u32[]{:S(2)}, u32[]{:S(2)}) collective-permute-start(f32[32,128]{1,0:T(8,128)S(1)} %get-tuple-element.101.own_ref), channel_id=1, source_target_pairs={{0,1},{1,0},{2,3},{3,2},{4,5},{5,4},{6,7},{7,6},{8,9},{9,8},{10,11... | collective-permute-start | bytes 49160 | tf_op jit(solution)/shard_map/ppermute | solution.py:272
  240.2 10.2 %all_to_all.94.parts_ref = f32[16,24,128]{2,1,0:T(8,128)S(1)} all-to-all(f32[16,24,128]{2,1,0:T(8,128)S(1)} %shard_map.90), channel_id=1, replica_groups=mesh['nodes_0'=4,'nodes_1'=8,'nodes_2'=4,'params'=2] {'nodes_0','nodes_2'}, dimensions={0} | all-to-all | bytes 393216 | tf_op jit(solution)/shard_map/all_to_all | solution.py:268
  250.4 10.0 %all_to_all.95.parts_ref = f32[8,24,128]{2,1,0:T(8,128)S(1)} all-to-all(f32[8,24,128]{2,1,0:T(8,128)S(1)} %shard_map.91), channel_id=1, replica_groups=mesh['nodes_0'=4,'nodes_1'=8,'nodes_2'=4,'params'=2] {'nodes_1'}, dimensions={0} | all-to-all | bytes 196608 | tf_op jit(solution)/shard_map/all_to_all | solution.py:268
  262.0 3.0 %collective-permute-start.11 = (f32[64,1024]{1,0:T(8,128)S(1)}, f32[64,1024]{1,0:T(8,128)S(1)}, u32[]{:S(2)}, u32[]{:S(2)}) collective-permute-start(f32[64,1024]{1,0:T(8,128)S(1)} %get-tuple-element.107.own_ref), channel_id=1, source_target_pairs={{0,1},{1,0},{2,3},{3,2},{4,5},{5,4},{6,7},{7,6},{8,9},{9,8},{10,11... | collective-permute-start | bytes 786440 | tf_op jit(solution)/shard_map/ppermute | solution.py:272
  (46 shorter events, 26.9 us)
Async XLA Ops:
  43.5 4.1 %collective-permute-start.1 = (f32[32,128]{1,0:T(8,128)S(1)}, f32[32,128]{1,0:T(8,128)S(1)}, u32[]{:S(2)}, u32[]{:S(2)}) collective-permute-start(f32[32,128]{1,0:T(8,128)S(1)} %get-tuple-element.62.own_ref), channel_id=1, source_target_pairs={{0,1},{1,0},{2,3},{3,2},{4,5},{5,4},{6,7},{7,6},{8,9},{9,8},{10,11... | collective-permute-start | bytes 49160 | tf_op jit(solution)/shard_map/ppermute | solution.py:272
  46.9 2.6 collective-permute-start
  71.2 4.8 %collective-permute-start.2 = (f32[64,1024]{1,0:T(8,128)S(1)}, f32[64,1024]{1,0:T(8,128)S(1)}, u32[]{:S(2)}, u32[]{:S(2)}) collective-permute-start(f32[64,1024]{1,0:T(8,128)S(1)} %get-tuple-element.68.own_ref), channel_id=1, source_target_pairs={{0,1},{1,0},{2,3},{3,2},{4,5},{5,4},{6,7},{7,6},{8,9},{9,8},{10,11... | collective-permute-start | bytes 786440 | tf_op jit(solution)/shard_map/ppermute | solution.py:272
  107.3 3.7 %collective-permute-start.4 = (f32[32,128]{1,0:T(8,128)S(1)}, f32[32,128]{1,0:T(8,128)S(1)}, u32[]{:S(2)}, u32[]{:S(2)}) collective-permute-start(f32[32,128]{1,0:T(8,128)S(1)} %get-tuple-element.75.own_ref), channel_id=1, source_target_pairs={{0,1},{1,0},{2,3},{3,2},{4,5},{5,4},{6,7},{7,6},{8,9},{9,8},{10,11... | collective-permute-start | bytes 49160 | tf_op jit(solution)/shard_map/ppermute | solution.py:272
  110.3 2.6 collective-permute-start.3
  134.7 4.9 %collective-permute-start.5 = (f32[64,1024]{1,0:T(8,128)S(1)}, f32[64,1024]{1,0:T(8,128)S(1)}, u32[]{:S(2)}, u32[]{:S(2)}) collective-permute-start(f32[64,1024]{1,0:T(8,128)S(1)} %get-tuple-element.81.own_ref), channel_id=1, source_target_pairs={{0,1},{1,0},{2,3},{3,2},{4,5},{5,4},{6,7},{7,6},{8,9},{9,8},{10,11... | collective-permute-start | bytes 786440 | tf_op jit(solution)/shard_map/ppermute | solution.py:272
  170.8 3.7 %collective-permute-start.7 = (f32[32,128]{1,0:T(8,128)S(1)}, f32[32,128]{1,0:T(8,128)S(1)}, u32[]{:S(2)}, u32[]{:S(2)}) collective-permute-start(f32[32,128]{1,0:T(8,128)S(1)} %get-tuple-element.88.own_ref), channel_id=1, source_target_pairs={{0,1},{1,0},{2,3},{3,2},{4,5},{5,4},{6,7},{7,6},{8,9},{9,8},{10,11... | collective-permute-start | bytes 49160 | tf_op jit(solution)/shard_map/ppermute | solution.py:272
  173.9 2.6 collective-permute-start.6
  198.2 5.1 %collective-permute-start.8 = (f32[64,1024]{1,0:T(8,128)S(1)}, f32[64,1024]{1,0:T(8,128)S(1)}, u32[]{:S(2)}, u32[]{:S(2)}) collective-permute-start(f32[64,1024]{1,0:T(8,128)S(1)} %get-tuple-element.94.own_ref), channel_id=1, source_target_pairs={{0,1},{1,0},{2,3},{3,2},{4,5},{5,4},{6,7},{7,6},{8,9},{9,8},{10,11... | collective-permute-start | bytes 786440 | tf_op jit(solution)/shard_map/ppermute | solution.py:272
  234.6 3.7 %collective-permute-start.10 = (f32[32,128]{1,0:T(8,128)S(1)}, f32[32,128]{1,0:T(8,128)S(1)}, u32[]{:S(2)}, u32[]{:S(2)}) collective-permute-start(f32[32,128]{1,0:T(8,128)S(1)} %get-tuple-element.101.own_ref), channel_id=1, source_target_pairs={{0,1},{1,0},{2,3},{3,2},{4,5},{5,4},{6,7},{7,6},{8,9},{9,8},{10,11... | collective-permute-start | bytes 49160 | tf_op jit(solution)/shard_map/ppermute | solution.py:272
  237.6 2.6 collective-permute-start.9
  262.0 5.5 %collective-permute-start.11 = (f32[64,1024]{1,0:T(8,128)S(1)}, f32[64,1024]{1,0:T(8,128)S(1)}, u32[]{:S(2)}, u32[]{:S(2)}) collective-permute-start(f32[64,1024]{1,0:T(8,128)S(1)} %get-tuple-element.107.own_ref), channel_id=1, source_target_pairs={{0,1},{1,0},{2,3},{3,2},{4,5},{5,4},{6,7},{7,6},{8,9},{9,8},{10,11... | collective-permute-start | bytes 786440 | tf_op jit(solution)/shard_map/ppermute | solution.py:272

commit v2 on v1

--- a/solution.py
+++ b/solution.py
@@ -14,7 +14,8 @@
 LINE = "nodes_1"
 CORE = "params"
 GROUP = 8
-GROUPS = 2
+CHUNK = 2
+WHOLE = 8
 F32 = jnp.float32
 BF16 = jnp.bfloat16
 EXACT = lax.Precision.HIGHEST
@@ -123,7 +124,7 @@
         ref[i, rows, :] = x
 
 
-def contract(rows_ref, space, times, contracted_ref, message_ref, side_ref, arrive=None):
+def contract(rows_ref, space, times, contracted_ref, message_ref, side_ref, groups_at_once, arrive=None):
     steps, rank = times.shape
     samples = side_ref.shape[0]
     low = space.astype(BF16)
@@ -135,8 +136,8 @@
     def groups(step, carry):
         if arrive is not None:
             arrive(step)
-        for group in range(GROUPS):
-            first = pl.multiple_of((step * GROUPS + group) * GROUP, GROUP)
+        for group in range(groups_at_once):
+            first = pl.multiple_of((step * groups_at_once + group) * GROUP, GROUP)
             here = pl.ds(pl.multiple_of(first * steps, GROUP * steps), GROUP * steps)
             part = dot(rows_ref[here, :], low, (1, 1))
             contracted_ref[here, :] = part
@@ -146,7 +147,7 @@
             side_ref[pl.ds(first, GROUP), :] = jnp.concatenate(sides, axis=0)
         return carry
 
-    lax.fori_loop(0, samples // (GROUP * GROUPS), groups, 0)
+    lax.fori_loop(0, samples // (GROUP * groups_at_once), groups, 0)
     spread(message_ref, fold(side_ref[...]), slice(0, samples // 2))
 
 
@@ -183,13 +184,20 @@
         copy.wait()
     gram_ref[...] = gram_rows(times_here[...])
     contract(
-        rows_ref, space_here[...], times_here[...], contracted_ref, message_ref, side_ref, lambda step: load(step).wait()
+        rows_ref,
+        space_here[...],
+        times_here[...],
+        contracted_ref,
+        message_ref,
+        side_ref,
+        CHUNK,
+        lambda step: load(step).wait(),
     )
 
 
 def space_kernel(rows_ref, own_ref, other_ref, inverse_ref, times_ref, contracted_ref, message_ref, side_ref):
     space = dot(inverse_ref[...], own_ref[...] + other_ref[...], (1, 0), EXACT)
-    contract(rows_ref, space, times_ref[...], contracted_ref, message_ref, side_ref)
+    contract(rows_ref, space, times_ref[...], contracted_ref, message_ref, side_ref, WHOLE)
 
 
 def last_kernel(own_ref, other_ref, inverse_ref, space_ref):
@@ -290,7 +298,7 @@
             pltpu.VMEM((samples, rank), F32),
             pltpu.VMEM((rank, nodes), F32),
             pltpu.VMEM((steps, rank), F32),
-            pltpu.SemaphoreType.DMA((samples // (GROUP * GROUPS),)),
+            pltpu.SemaphoreType.DMA((samples // (GROUP * CHUNK),)),
             pltpu.SemaphoreType.DMA((2,)),
         ],
         24,

time: 269 us -> 280 us (1.041); the launches traced: 269 us -> 275 us
  blocking collectives: 190 us -> 198 us
    all_to_all x16, blocking collectives: 190 us -> 198 us  [exchange(): return lax.all_to_all(copies, axes, split_axis=0, concat_axis=0, tiled=True)]
where the time goes in v2:
time: 280 us; the launch traced here: 275 us
  blocking collectives  198 us (71%)
  Pallas kernels  48.5 us (17%)
  starting transfers between devices  24.1 us (9%)
    all_to_all x16, blocking collectives, exchange(): return lax.all_to_all(copies, axes, split_axis=0, concat_axis=0, tiled=True)  198 us
    ppermute x12, starting transfers between devices, other_core(): return lax.ppermute(x, CORE, [(0, 1), (1, 0)])  24.1 us
    pallas_call x4, Pallas kernels, per_device(): params, gram, space_gram = for_params(exchange(message, LINE), time_gram)  12.7 us
    pallas_call x4, Pallas kernels, per_device(): inverse, param_gram = times_inverse(gram, other_gram, space_gram)  7.7 us
    pallas_call x4, Pallas kernels, per_device(): inverse, = space_inverse(param_gram, time_gram)  7.53 us
    pallas_call x3, Pallas kernels, per_device(): contracted, message = again(rows, side, other, inverse, times)  6.96 us
    pallas_call x4, Pallas kernels, per_device(): for_times(rows, exchange(message, LINE), inverse, params)  6.25 us
  transfers between devices with their start and end apart: 12, of which 4 were waited for; matrix products, arithmetic and copies ran while one was open for 0% of the time, Pallas kernels for 6%

profile of v2, /device:TPU:1, one launch (start us, length us, event | category | flops | bytes accessed | tf_op | source)
XLA Modules:
  0.0 274.8 jit_solution(6176666070849487777)
XLA Ops:
  0.6 5.3 %shard_map.58 = (bf16[3072,1024]{1,0:T(8,128)(2,1)S(1)}, f32[3072,64]{1,0:T(8,128)S(1)}, f32[16,49,128]{2,1,0:T(8,128)S(1)}, f32[64,64]{1,0:T(8,128)S(1)}) custom-call(bf16[3072,1024]{1,0:T(8,128)(2,1)} %bitcast.5, f32[64,1024]{1,0:T(8,128)} %space_ref.1, f32[48,64]{1,0:T(8,128)} %bitcast.6), custom_call_target="tpu_custom_call" | custom-call | tf_op jit(solution)/shard_map/pallas_call | solution.py:321
  5.9 17.3 %all_to_all.80.parts_ref = f32[16,49,128]{2,1,0:T(8,128)S(1)} all-to-all(f32[16,49,128]{2,1,0:T(8,128)S(1)} %get-tuple-element.59), channel_id=1, replica_groups=mesh['nodes_0'=4,'nodes_1'=8,'nodes_2'=4,'params'=2] {'nodes_0','nodes_2'}, dimensions={0} | all-to-all | bytes 802816 | tf_op jit(solution)/shard_map/all_to_all | solution.py:276
  23.2 17.1 %all_to_all.81.parts_ref = f32[8,49,128]{2,1,0:T(8,128)S(1)} all-to-all(f32[8,49,128]{2,1,0:T(8,128)S(1)} %shard_map.59), channel_id=1, replica_groups=mesh['nodes_0'=4,'nodes_1'=8,'nodes_2'=4,'params'=2] {'nodes_1'}, dimensions={0} | all-to-all | bytes 401408 | tf_op jit(solution)/shard_map/all_to_all | solution.py:276
  40.3 3.2 %shard_map.60 = (f32[64,64]{1,0:T(8,128)S(1)}, f32[32,128]{1,0:T(8,128)S(1)}, f32[64,64]{1,0:T(8,128)S(1)}) custom-call(f32[8,49,128]{2,1,0:T(8,128)S(1)} %all_to_all.81.parts_ref, f32[64,64]{1,0:T(8,128)S(1)} %get-tuple-element.60.time_gram_ref), custom_call_target="tpu_custom_call" | custom-call | tf_op jit(solution)/shard_map/pallas_call | solution.py:324
  43.5 3.2 %collective-permute-start.1 = (f32[32,128]{1,0:T(8,128)S(1)}, f32[32,128]{1,0:T(8,128)S(1)}, u32[]{:S(2)}, u32[]{:S(2)}) collective-permute-start(f32[32,128]{1,0:T(8,128)S(1)} %get-tuple-element.62.own_ref), channel_id=1, source_target_pairs={{0,1},{1,0},{2,3},{3,2},{4,5},{5,4},{6,7},{7,6},{8,9},{9,8},{10,11... | collective-permute-start | bytes 49160 | tf_op jit(solution)/shard_map/ppermute | solution.py:280
  49.5 10.1 %all_to_all.82.parts_ref = f32[16,24,128]{2,1,0:T(8,128)S(1)} all-to-all(f32[16,24,128]{2,1,0:T(8,128)S(1)} %shard_map.63), channel_id=1, replica_groups=mesh['nodes_0'=4,'nodes_1'=8,'nodes_2'=4,'params'=2] {'nodes_0','nodes_2'}, dimensions={0} | all-to-all | bytes 393216 | tf_op jit(solution)/shard_map/all_to_all | solution.py:276
  59.6 10.0 %all_to_all.83.parts_ref = f32[8,24,128]{2,1,0:T(8,128)S(1)} all-to-all(f32[8,24,128]{2,1,0:T(8,128)S(1)} %shard_map.64), channel_id=1, replica_groups=mesh['nodes_0'=4,'nodes_1'=8,'nodes_2'=4,'params'=2] {'nodes_1'}, dimensions={0} | all-to-all | bytes 196608 | tf_op jit(solution)/shard_map/all_to_all | solution.py:276
  71.2 3.0 %collective-permute-start.2 = (f32[64,1024]{1,0:T(8,128)S(1)}, f32[64,1024]{1,0:T(8,128)S(1)}, u32[]{:S(2)}, u32[]{:S(2)}) collective-permute-start(f32[64,1024]{1,0:T(8,128)S(1)} %get-tuple-element.68.own_ref), channel_id=1, source_target_pairs={{0,1},{1,0},{2,3},{3,2},{4,5},{5,4},{6,7},{7,6},{8,9},{9,8},{10,11... | collective-permute-start | bytes 786440 | tf_op jit(solution)/shard_map/ppermute | solution.py:280
  76.0 2.3 shard_map.67
  78.4 13.1 %all_to_all.84.parts_ref = f32[16,49,128]{2,1,0:T(8,128)S(1)} all-to-all(f32[16,49,128]{2,1,0:T(8,128)S(1)} %get-tuple-element.73), channel_id=1, replica_groups=mesh['nodes_0'=4,'nodes_1'=8,'nodes_2'=4,'params'=2] {'nodes_0','nodes_2'}, dimensions={0} | all-to-all | bytes 802816 | tf_op jit(solution)/shard_map/all_to_all | solution.py:276
  91.5 11.8 %all_to_all.85.parts_ref = f32[8,49,128]{2,1,0:T(8,128)S(1)} all-to-all(f32[8,49,128]{2,1,0:T(8,128)S(1)} %shard_map.68), channel_id=1, replica_groups=mesh['nodes_0'=4,'nodes_1'=8,'nodes_2'=4,'params'=2] {'nodes_1'}, dimensions={0} | all-to-all | bytes 401408 | tf_op jit(solution)/shard_map/all_to_all | solution.py:276
  103.3 3.2 %shard_map.69 = (f32[64,64]{1,0:T(8,128)S(1)}, f32[32,128]{1,0:T(8,128)S(1)}, f32[64,64]{1,0:T(8,128)S(1)}) custom-call(f32[8,49,128]{2,1,0:T(8,128)S(1)} %all_to_all.85.parts_ref, f32[64,64]{1,0:T(8,128)S(1)} %get-tuple-element.70.second_ref.time_gram_ref), custom_call_target="tpu_custom_call" | custom-call | tf_op jit(solution)/shard_map/pallas_call | solution.py:324
  106.4 3.1 %collective-permute-start.4 = (f32[32,128]{1,0:T(8,128)S(1)}, f32[32,128]{1,0:T(8,128)S(1)}, u32[]{:S(2)}, u32[]{:S(2)}) collective-permute-start(f32[32,128]{1,0:T(8,128)S(1)} %get-tuple-element.75.own_ref), channel_id=1, source_target_pairs={{0,1},{1,0},{2,3},{3,2},{4,5},{5,4},{6,7},{7,6},{8,9},{9,8},{10,11... | collective-permute-start | bytes 49160 | tf_op jit(solution)/shard_map/ppermute | solution.py:280
  112.3 10.2 %all_to_all.86.parts_ref = f32[16,24,128]{2,1,0:T(8,128)S(1)} all-to-all(f32[16,24,128]{2,1,0:T(8,128)S(1)} %shard_map.72), channel_id=1, replica_groups=mesh['nodes_0'=4,'nodes_1'=8,'nodes_2'=4,'params'=2] {'nodes_0','nodes_2'}, dimensions={0} | all-to-all | bytes 393216 | tf_op jit(solution)/shard_map/all_to_all | solution.py:276
  122.5 10.0 %all_to_all.87.parts_ref = f32[8,24,128]{2,1,0:T(8,128)S(1)} all-to-all(f32[8,24,128]{2,1,0:T(8,128)S(1)} %shard_map.73), channel_id=1, replica_groups=mesh['nodes_0'=4,'nodes_1'=8,'nodes_2'=4,'params'=2] {'nodes_1'}, dimensions={0} | all-to-all | bytes 196608 | tf_op jit(solution)/shard_map/all_to_all | solution.py:276
  134.1 3.0 %collective-permute-start.5 = (f32[64,1024]{1,0:T(8,128)S(1)}, f32[64,1024]{1,0:T(8,128)S(1)}, u32[]{:S(2)}, u32[]{:S(2)}) collective-permute-start(f32[64,1024]{1,0:T(8,128)S(1)} %get-tuple-element.81.own_ref), channel_id=1, source_target_pairs={{0,1},{1,0},{2,3},{3,2},{4,5},{5,4},{6,7},{7,6},{8,9},{9,8},{10,11... | collective-permute-start | bytes 786440 | tf_op jit(solution)/shard_map/ppermute | solution.py:280
  138.9 2.3 shard_map.76
  141.2 13.1 %all_to_all.88.parts_ref = f32[16,49,128]{2,1,0:T(8,128)S(1)} all-to-all(f32[16,49,128]{2,1,0:T(8,128)S(1)} %get-tuple-element.86), channel_id=1, replica_groups=mesh['nodes_0'=4,'nodes_1'=8,'nodes_2'=4,'params'=2] {'nodes_0','nodes_2'}, dimensions={0} | all-to-all | bytes 802816 | tf_op jit(solution)/shard_map/all_to_all | solution.py:276
  154.3 11.8 %all_to_all.89.parts_ref = f32[8,49,128]{2,1,0:T(8,128)S(1)} all-to-all(f32[8,49,128]{2,1,0:T(8,128)S(1)} %shard_map.77), channel_id=1, replica_groups=mesh['nodes_0'=4,'nodes_1'=8,'nodes_2'=4,'params'=2] {'nodes_1'}, dimensions={0} | all-to-all | bytes 401408 | tf_op jit(solution)/shard_map/all_to_all | solution.py:276
  166.1 3.2 %shard_map.78 = (f32[64,64]{1,0:T(8,128)S(1)}, f32[32,128]{1,0:T(8,128)S(1)}, f32[64,64]{1,0:T(8,128)S(1)}) custom-call(f32[8,49,128]{2,1,0:T(8,128)S(1)} %all_to_all.89.parts_ref, f32[64,64]{1,0:T(8,128)S(1)} %get-tuple-element.83.second_ref.time_gram_ref), custom_call_target="tpu_custom_call" | custom-call | tf_op jit(solution)/shard_map/pallas_call | solution.py:324
  169.3 2.8 %collective-permute-start.7 = (f32[32,128]{1,0:T(8,128)S(1)}, f32[32,128]{1,0:T(8,128)S(1)}, u32[]{:S(2)}, u32[]{:S(2)}) collective-permute-start(f32[32,128]{1,0:T(8,128)S(1)} %get-tuple-element.88.own_ref), channel_id=1, source_target_pairs={{0,1},{1,0},{2,3},{3,2},{4,5},{5,4},{6,7},{7,6},{8,9},{9,8},{10,11... | collective-permute-start | bytes 49160 | tf_op jit(solution)/shard_map/ppermute | solution.py:280
  174.9 10.2 %all_to_all.90.parts_ref = f32[16,24,128]{2,1,0:T(8,128)S(1)} all-to-all(f32[16,24,128]{2,1,0:T(8,128)S(1)} %shard_map.81), channel_id=1, replica_groups=mesh['nodes_0'=4,'nodes_1'=8,'nodes_2'=4,'params'=2] {'nodes_0','nodes_2'}, dimensions={0} | all-to-all | bytes 393216 | tf_op jit(solution)/shard_map/all_to_all | solution.py:276
  185.1 18.6 %all_to_all.91.parts_ref = f32[8,24,128]{2,1,0:T(8,128)S(1)} all-to-all(f32[8,24,128]{2,1,0:T(8,128)S(1)} %shard_map.82), channel_id=1, replica_groups=mesh['nodes_0'=4,'nodes_1'=8,'nodes_2'=4,'params'=2] {'nodes_1'}, dimensions={0} | all-to-all | bytes 196608 | tf_op jit(solution)/shard_map/all_to_all | solution.py:276
  205.3 3.0 %collective-permute-start.8 = (f32[64,1024]{1,0:T(8,128)S(1)}, f32[64,1024]{1,0:T(8,128)S(1)}, u32[]{:S(2)}, u32[]{:S(2)}) collective-permute-start(f32[64,1024]{1,0:T(8,128)S(1)} %get-tuple-element.94.own_ref), channel_id=1, source_target_pairs={{0,1},{1,0},{2,3},{3,2},{4,5},{5,4},{6,7},{7,6},{8,9},{9,8},{10,11... | collective-permute-start | bytes 786440 | tf_op jit(solution)/shard_map/ppermute | solution.py:280
  210.2 2.3 shard_map.85
  212.5 13.1 %all_to_all.92.parts_ref = f32[16,49,128]{2,1,0:T(8,128)S(1)} all-to-all(f32[16,49,128]{2,1,0:T(8,128)S(1)} %get-tuple-element.99), channel_id=1, replica_groups=mesh['nodes_0'=4,'nodes_1'=8,'nodes_2'=4,'params'=2] {'nodes_0','nodes_2'}, dimensions={0} | all-to-all | bytes 802816 | tf_op jit(solution)/shard_map/all_to_all | solution.py:276
  225.6 11.8 %all_to_all.93.parts_ref = f32[8,49,128]{2,1,0:T(8,128)S(1)} all-to-all(f32[8,49,128]{2,1,0:T(8,128)S(1)} %shard_map.86), channel_id=1, replica_groups=mesh['nodes_0'=4,'nodes_1'=8,'nodes_2'=4,'params'=2] {'nodes_1'}, dimensions={0} | all-to-all | bytes 401408 | tf_op jit(solution)/shard_map/all_to_all | solution.py:276
  237.4 3.2 %shard_map.87 = (f32[64,64]{1,0:T(8,128)S(1)}, f32[32,128]{1,0:T(8,128)S(1)}, f32[64,64]{1,0:T(8,128)S(1)}) custom-call(f32[8,49,128]{2,1,0:T(8,128)S(1)} %all_to_all.93.parts_ref, f32[64,64]{1,0:T(8,128)S(1)} %get-tuple-element.96.second_ref.time_gram_ref), custom_call_target="tpu_custom_call" | custom-call | tf_op jit(solution)/shard_map/pallas_call | solution.py:324
  240.6 2.8 %collective-permute-start.10 = (f32[32,128]{1,0:T(8,128)S(1)}, f32[32,128]{1,0:T(8,128)S(1)}, u32[]{:S(2)}, u32[]{:S(2)}) collective-permute-start(f32[32,128]{1,0:T(8,128)S(1)} %get-tuple-element.101.own_ref), channel_id=1, source_target_pairs={{0,1},{1,0},{2,3},{3,2},{4,5},{5,4},{6,7},{7,6},{8,9},{9,8},{10,11... | collective-permute-start | bytes 49160 | tf_op jit(solution)/shard_map/ppermute | solution.py:280
  246.2 10.2 %all_to_all.94.parts_ref = f32[16,24,128]{2,1,0:T(8,128)S(1)} all-to-all(f32[16,24,128]{2,1,0:T(8,128)S(1)} %shard_map.90), channel_id=1, replica_groups=mesh['nodes_0'=4,'nodes_1'=8,'nodes_2'=4,'params'=2] {'nodes_0','nodes_2'}, dimensions={0} | all-to-all | bytes 393216 | tf_op jit(solution)/shard_map/all_to_all | solution.py:276
  256.4 10.0 %all_to_all.95.parts_ref = f32[8,24,128]{2,1,0:T(8,128)S(1)} all-to-all(f32[8,24,128]{2,1,0:T(8,128)S(1)} %shard_map.91), channel_id=1, replica_groups=mesh['nodes_0'=4,'nodes_1'=8,'nodes_2'=4,'params'=2] {'nodes_1'}, dimensions={0} | all-to-all | bytes 196608 | tf_op jit(solution)/shard_map/all_to_all | solution.py:276
  268.0 3.0 %collective-permute-start.11 = (f32[64,1024]{1,0:T(8,128)S(1)}, f32[64,1024]{1,0:T(8,128)S(1)}, u32[]{:S(2)}, u32[]{:S(2)}) collective-permute-start(f32[64,1024]{1,0:T(8,128)S(1)} %get-tuple-element.107.own_ref), channel_id=1, source_target_pairs={{0,1},{1,0},{2,3},{3,2},{4,5},{5,4},{6,7},{7,6},{8,9},{9,8},{10,11... | collective-permute-start | bytes 786440 | tf_op jit(solution)/shard_map/ppermute | solution.py:280
  (46 shorter events, 26.9 us)
Async XLA Ops:
  43.5 4.1 %collective-permute-start.1 = (f32[32,128]{1,0:T(8,128)S(1)}, f32[32,128]{1,0:T(8,128)S(1)}, u32[]{:S(2)}, u32[]{:S(2)}) collective-permute-start(f32[32,128]{1,0:T(8,128)S(1)} %get-tuple-element.62.own_ref), channel_id=1, source_target_pairs={{0,1},{1,0},{2,3},{3,2},{4,5},{5,4},{6,7},{7,6},{8,9},{9,8},{10,11... | collective-permute-start | bytes 49160 | tf_op jit(solution)/shard_map/ppermute | solution.py:280
  46.9 2.6 collective-permute-start
  71.2 4.8 %collective-permute-start.2 = (f32[64,1024]{1,0:T(8,128)S(1)}, f32[64,1024]{1,0:T(8,128)S(1)}, u32[]{:S(2)}, u32[]{:S(2)}) collective-permute-start(f32[64,1024]{1,0:T(8,128)S(1)} %get-tuple-element.68.own_ref), channel_id=1, source_target_pairs={{0,1},{1,0},{2,3},{3,2},{4,5},{5,4},{6,7},{7,6},{8,9},{9,8},{10,11... | collective-permute-start | bytes 786440 | tf_op jit(solution)/shard_map/ppermute | solution.py:280
  106.4 3.9 %collective-permute-start.4 = (f32[32,128]{1,0:T(8,128)S(1)}, f32[32,128]{1,0:T(8,128)S(1)}, u32[]{:S(2)}, u32[]{:S(2)}) collective-permute-start(f32[32,128]{1,0:T(8,128)S(1)} %get-tuple-element.75.own_ref), channel_id=1, source_target_pairs={{0,1},{1,0},{2,3},{3,2},{4,5},{5,4},{6,7},{7,6},{8,9},{9,8},{10,11... | collective-permute-start | bytes 49160 | tf_op jit(solution)/shard_map/ppermute | solution.py:280
  109.7 2.6 collective-permute-start.3
  134.1 4.9 %collective-permute-start.5 = (f32[64,1024]{1,0:T(8,128)S(1)}, f32[64,1024]{1,0:T(8,128)S(1)}, u32[]{:S(2)}, u32[]{:S(2)}) collective-permute-start(f32[64,1024]{1,0:T(8,128)S(1)} %get-tuple-element.81.own_ref), channel_id=1, source_target_pairs={{0,1},{1,0},{2,3},{3,2},{4,5},{5,4},{6,7},{7,6},{8,9},{9,8},{10,11... | collective-permute-start | bytes 786440 | tf_op jit(solution)/shard_map/ppermute | solution.py:280
  169.3 3.7 %collective-permute-start.7 = (f32[32,128]{1,0:T(8,128)S(1)}, f32[32,128]{1,0:T(8,128)S(1)}, u32[]{:S(2)}, u32[]{:S(2)}) collective-permute-start(f32[32,128]{1,0:T(8,128)S(1)} %get-tuple-element.88.own_ref), channel_id=1, source_target_pairs={{0,1},{1,0},{2,3},{3,2},{4,5},{5,4},{6,7},{7,6},{8,9},{9,8},{10,11... | collective-permute-start | bytes 49160 | tf_op jit(solution)/shard_map/ppermute | solution.py:280
  172.3 2.6 collective-permute-start.6
  205.3 4.9 %collective-permute-start.8 = (f32[64,1024]{1,0:T(8,128)S(1)}, f32[64,1024]{1,0:T(8,128)S(1)}, u32[]{:S(2)}, u32[]{:S(2)}) collective-permute-start(f32[64,1024]{1,0:T(8,128)S(1)} %get-tuple-element.94.own_ref), channel_id=1, source_target_pairs={{0,1},{1,0},{2,3},{3,2},{4,5},{5,4},{6,7},{7,6},{8,9},{9,8},{10,11... | collective-permute-start | bytes 786440 | tf_op jit(solution)/shard_map/ppermute | solution.py:280
  240.6 3.7 %collective-permute-start.10 = (f32[32,128]{1,0:T(8,128)S(1)}, f32[32,128]{1,0:T(8,128)S(1)}, u32[]{:S(2)}, u32[]{:S(2)}) collective-permute-start(f32[32,128]{1,0:T(8,128)S(1)} %get-tuple-element.101.own_ref), channel_id=1, source_target_pairs={{0,1},{1,0},{2,3},{3,2},{4,5},{5,4},{6,7},{7,6},{8,9},{9,8},{10,11... | collective-permute-start | bytes 49160 | tf_op jit(solution)/shard_map/ppermute | solution.py:280
  243.6 2.6 collective-permute-start.9
  268.0 5.5 %collective-permute-start.11 = (f32[64,1024]{1,0:T(8,128)S(1)}, f32[64,1024]{1,0:T(8,128)S(1)}, u32[]{:S(2)}, u32[]{:S(2)}) collective-permute-start(f32[64,1024]{1,0:T(8,128)S(1)} %get-tuple-element.107.own_ref), channel_id=1, source_target_pairs={{0,1},{1,0},{2,3},{3,2},{4,5},{5,4},{6,7},{7,6},{8,9},{9,8},{10,11... | collective-permute-start | bytes 786440 | tf_op jit(solution)/shard_map/ppermute | solution.py:280

commit v3 on v2

--- a/solution.py
+++ b/solution.py
@@ -15,7 +15,7 @@
 CORE = "params"
 GROUP = 8
 CHUNK = 2
-WHOLE = 8
+WHOLE = 4
 F32 = jnp.float32
 BF16 = jnp.bfloat16
 EXACT = lax.Precision.HIGHEST

time: 280 us -> 268 us (0.957); the launches traced: 275 us -> 268 us
  blocking collectives: 198 us -> 190 us
    all_to_all x16, blocking collectives: 198 us -> 190 us  [exchange(): return lax.all_to_all(copies, axes, split_axis=0, concat_axis=0, tiled=True)]
where the time goes in v3:
time: 268 us
  blocking collectives  190 us (71%)
  Pallas kernels  50.3 us (19%)
  starting transfers between devices  24.3 us (9%)
    all_to_all x16, blocking collectives, exchange(): return lax.all_to_all(copies, axes, split_axis=0, concat_axis=0, tiled=True)  190 us
    ppermute x12, starting transfers between devices, other_core(): return lax.ppermute(x, CORE, [(0, 1), (1, 0)])  24.3 us
    pallas_call x4, Pallas kernels, per_device(): params, gram, space_gram = for_params(exchange(message, LINE), time_gram)  12.7 us
    pallas_call x3, Pallas kernels, per_device(): contracted, message = again(rows, side, other, inverse, times)  8.79 us
    pallas_call x4, Pallas kernels, per_device(): inverse, param_gram = times_inverse(gram, other_gram, space_gram)  7.7 us
    pallas_call x4, Pallas kernels, per_device(): inverse, = space_inverse(param_gram, time_gram)  7.53 us
    pallas_call x4, Pallas kernels, per_device(): for_times(rows, exchange(message, LINE), inverse, params)  6.24 us
  transfers between devices with their start and end apart: 12, of which 4 were waited for; matrix products, arithmetic and copies ran while one was open for 0% of the time, Pallas kernels for 6%

profile of v3, /device:TPU:1, one launch (start us, length us, event | category | flops | bytes accessed | tf_op | source)
XLA Modules:
  0.0 267.7 jit_solution(11561821258315456800)
XLA Ops:
  0.6 5.3 %shard_map.58 = (bf16[3072,1024]{1,0:T(8,128)(2,1)S(1)}, f32[3072,64]{1,0:T(8,128)S(1)}, f32[16,49,128]{2,1,0:T(8,128)S(1)}, f32[64,64]{1,0:T(8,128)S(1)}) custom-call(bf16[3072,1024]{1,0:T(8,128)(2,1)} %bitcast.5, f32[64,1024]{1,0:T(8,128)} %space_ref.1, f32[48,64]{1,0:T(8,128)} %bitcast.6), custom_call_target="tpu_custom_call" | custom-call | tf_op jit(solution)/shard_map/pallas_call | solution.py:321
  5.9 17.3 %all_to_all.80.parts_ref = f32[16,49,128]{2,1,0:T(8,128)S(1)} all-to-all(f32[16,49,128]{2,1,0:T(8,128)S(1)} %get-tuple-element.59), channel_id=1, replica_groups=mesh['nodes_0'=4,'nodes_1'=8,'nodes_2'=4,'params'=2] {'nodes_0','nodes_2'}, dimensions={0} | all-to-all | bytes 802816 | tf_op jit(solution)/shard_map/all_to_all | solution.py:276
  23.2 17.1 %all_to_all.81.parts_ref = f32[8,49,128]{2,1,0:T(8,128)S(1)} all-to-all(f32[8,49,128]{2,1,0:T(8,128)S(1)} %shard_map.59), channel_id=1, replica_groups=mesh['nodes_0'=4,'nodes_1'=8,'nodes_2'=4,'params'=2] {'nodes_1'}, dimensions={0} | all-to-all | bytes 401408 | tf_op jit(solution)/shard_map/all_to_all | solution.py:276
  40.3 3.2 %shard_map.60 = (f32[64,64]{1,0:T(8,128)S(1)}, f32[32,128]{1,0:T(8,128)S(1)}, f32[64,64]{1,0:T(8,128)S(1)}) custom-call(f32[8,49,128]{2,1,0:T(8,128)S(1)} %all_to_all.81.parts_ref, f32[64,64]{1,0:T(8,128)S(1)} %get-tuple-element.60.time_gram_ref), custom_call_target="tpu_custom_call" | custom-call | tf_op jit(solution)/shard_map/pallas_call | solution.py:324
  43.5 3.2 %collective-permute-start.1 = (f32[32,128]{1,0:T(8,128)S(1)}, f32[32,128]{1,0:T(8,128)S(1)}, u32[]{:S(2)}, u32[]{:S(2)}) collective-permute-start(f32[32,128]{1,0:T(8,128)S(1)} %get-tuple-element.62.own_ref), channel_id=1, source_target_pairs={{0,1},{1,0},{2,3},{3,2},{4,5},{5,4},{6,7},{7,6},{8,9},{9,8},{10,11... | collective-permute-start | bytes 49160 | tf_op jit(solution)/shard_map/ppermute | solution.py:280
  49.5 10.1 %all_to_all.82.parts_ref = f32[16,24,128]{2,1,0:T(8,128)S(1)} all-to-all(f32[16,24,128]{2,1,0:T(8,128)S(1)} %shard_map.63), channel_id=1, replica_groups=mesh['nodes_0'=4,'nodes_1'=8,'nodes_2'=4,'params'=2] {'nodes_0','nodes_2'}, dimensions={0} | all-to-all | bytes 393216 | tf_op jit(solution)/shard_map/all_to_all | solution.py:276
  59.6 10.0 %all_to_all.83.parts_ref = f32[8,24,128]{2,1,0:T(8,128)S(1)} all-to-all(f32[8,24,128]{2,1,0:T(8,128)S(1)} %shard_map.64), channel_id=1, replica_groups=mesh['nodes_0'=4,'nodes_1'=8,'nodes_2'=4,'params'=2] {'nodes_1'}, dimensions={0} | all-to-all | bytes 196608 | tf_op jit(solution)/shard_map/all_to_all | solution.py:276
  71.2 3.0 %collective-permute-start.2 = (f32[64,1024]{1,0:T(8,128)S(1)}, f32[64,1024]{1,0:T(8,128)S(1)}, u32[]{:S(2)}, u32[]{:S(2)}) collective-permute-start(f32[64,1024]{1,0:T(8,128)S(1)} %get-tuple-element.68.own_ref), channel_id=1, source_target_pairs={{0,1},{1,0},{2,3},{3,2},{4,5},{5,4},{6,7},{7,6},{8,9},{9,8},{10,11... | collective-permute-start | bytes 786440 | tf_op jit(solution)/shard_map/ppermute | solution.py:280
  76.0 2.9 %shard_map.67 = (f32[3072,64]{1,0:T(8,128)S(1)}, f32[16,49,128]{2,1,0:T(8,128)S(1)}) custom-call(bf16[3072,1024]{1,0:T(8,128)(2,1)S(1)} %get-tuple-element.57.rows_ref, f32[64,1024]{1,0:T(8,128)S(1)} %get-tuple-element.68.own_ref, f32[64,1024]{1,0:T(8,128)S(1)} %collective-permute-done.2.other_ref, f32[64,64]{1,0:T(8,128)S(1)} %shard_map.66.inverse_ref, ...), custom_call_target="tpu_custom_call" | custom-call | tf_op jit(solution)/shard_map/pallas_call | solution.py:336
  79.0 13.0 %all_to_all.84.parts_ref = f32[16,49,128]{2,1,0:T(8,128)S(1)} all-to-all(f32[16,49,128]{2,1,0:T(8,128)S(1)} %get-tuple-element.73), channel_id=1, replica_groups=mesh['nodes_0'=4,'nodes_1'=8,'nodes_2'=4,'params'=2] {'nodes_0','nodes_2'}, dimensions={0} | all-to-all | bytes 802816 | tf_op jit(solution)/shard_map/all_to_all | solution.py:276
  92.0 11.8 %all_to_all.85.parts_ref = f32[8,49,128]{2,1,0:T(8,128)S(1)} all-to-all(f32[8,49,128]{2,1,0:T(8,128)S(1)} %shard_map.68), channel_id=1, replica_groups=mesh['nodes_0'=4,'nodes_1'=8,'nodes_2'=4,'params'=2] {'nodes_1'}, dimensions={0} | all-to-all | bytes 401408 | tf_op jit(solution)/shard_map/all_to_all | solution.py:276
  103.8 3.2 %shard_map.69 = (f32[64,64]{1,0:T(8,128)S(1)}, f32[32,128]{1,0:T(8,128)S(1)}, f32[64,64]{1,0:T(8,128)S(1)}) custom-call(f32[8,49,128]{2,1,0:T(8,128)S(1)} %all_to_all.85.parts_ref, f32[64,64]{1,0:T(8,128)S(1)} %get-tuple-element.70.second_ref.time_gram_ref), custom_call_target="tpu_custom_call" | custom-call | tf_op jit(solution)/shard_map/pallas_call | solution.py:324
  107.0 2.8 %collective-permute-start.4 = (f32[32,128]{1,0:T(8,128)S(1)}, f32[32,128]{1,0:T(8,128)S(1)}, u32[]{:S(2)}, u32[]{:S(2)}) collective-permute-start(f32[32,128]{1,0:T(8,128)S(1)} %get-tuple-element.75.own_ref), channel_id=1, source_target_pairs={{0,1},{1,0},{2,3},{3,2},{4,5},{5,4},{6,7},{7,6},{8,9},{9,8},{10,11... | collective-permute-start | bytes 49160 | tf_op jit(solution)/shard_map/ppermute | solution.py:280
  112.6 10.2 %all_to_all.86.parts_ref = f32[16,24,128]{2,1,0:T(8,128)S(1)} all-to-all(f32[16,24,128]{2,1,0:T(8,128)S(1)} %shard_map.72), channel_id=1, replica_groups=mesh['nodes_0'=4,'nodes_1'=8,'nodes_2'=4,'params'=2] {'nodes_0','nodes_2'}, dimensions={0} | all-to-all | bytes 393216 | tf_op jit(solution)/shard_map/all_to_all | solution.py:276
  122.8 10.0 %all_to_all.87.parts_ref = f32[8,24,128]{2,1,0:T(8,128)S(1)} all-to-all(f32[8,24,128]{2,1,0:T(8,128)S(1)} %shard_map.73), channel_id=1, replica_groups=mesh['nodes_0'=4,'nodes_1'=8,'nodes_2'=4,'params'=2] {'nodes_1'}, dimensions={0} | all-to-all | bytes 196608 | tf_op jit(solution)/shard_map/all_to_all | solution.py:276
  134.4 3.0 %collective-permute-start.5 = (f32[64,1024]{1,0:T(8,128)S(1)}, f32[64,1024]{1,0:T(8,128)S(1)}, u32[]{:S(2)}, u32[]{:S(2)}) collective-permute-start(f32[64,1024]{1,0:T(8,128)S(1)} %get-tuple-element.81.own_ref), channel_id=1, source_target_pairs={{0,1},{1,0},{2,3},{3,2},{4,5},{5,4},{6,7},{7,6},{8,9},{9,8},{10,11... | collective-permute-start | bytes 786440 | tf_op jit(solution)/shard_map/ppermute | solution.py:280
  139.3 2.9 %shard_map.76 = (f32[3072,64]{1,0:T(8,128)S(1)}, f32[16,49,128]{2,1,0:T(8,128)S(1)}) custom-call(bf16[3072,1024]{1,0:T(8,128)(2,1)S(1)} %get-tuple-element.57.rows_ref, f32[64,1024]{1,0:T(8,128)S(1)} %get-tuple-element.81.own_ref, f32[64,1024]{1,0:T(8,128)S(1)} %collective-permute-done.5.other_ref, f32[64,64]{1,0:T(8,128)S(1)} %shard_map.75.inverse_ref, ...), custom_call_target="tpu_custom_call" | custom-call | tf_op jit(solution)/shard_map/pallas_call | solution.py:336
  142.2 13.0 %all_to_all.88.parts_ref = f32[16,49,128]{2,1,0:T(8,128)S(1)} all-to-all(f32[16,49,128]{2,1,0:T(8,128)S(1)} %get-tuple-element.86), channel_id=1, replica_groups=mesh['nodes_0'=4,'nodes_1'=8,'nodes_2'=4,'params'=2] {'nodes_0','nodes_2'}, dimensions={0} | all-to-all | bytes 802816 | tf_op jit(solution)/shard_map/all_to_all | solution.py:276
  155.3 11.8 %all_to_all.89.parts_ref = f32[8,49,128]{2,1,0:T(8,128)S(1)} all-to-all(f32[8,49,128]{2,1,0:T(8,128)S(1)} %shard_map.77), channel_id=1, replica_groups=mesh['nodes_0'=4,'nodes_1'=8,'nodes_2'=4,'params'=2] {'nodes_1'}, dimensions={0} | all-to-all | bytes 401408 | tf_op jit(solution)/shard_map/all_to_all | solution.py:276
  167.0 3.2 %shard_map.78 = (f32[64,64]{1,0:T(8,128)S(1)}, f32[32,128]{1,0:T(8,128)S(1)}, f32[64,64]{1,0:T(8,128)S(1)}) custom-call(f32[8,49,128]{2,1,0:T(8,128)S(1)} %all_to_all.89.parts_ref, f32[64,64]{1,0:T(8,128)S(1)} %get-tuple-element.83.second_ref.time_gram_ref), custom_call_target="tpu_custom_call" | custom-call | tf_op jit(solution)/shard_map/pallas_call | solution.py:324
  170.2 2.8 %collective-permute-start.7 = (f32[32,128]{1,0:T(8,128)S(1)}, f32[32,128]{1,0:T(8,128)S(1)}, u32[]{:S(2)}, u32[]{:S(2)}) collective-permute-start(f32[32,128]{1,0:T(8,128)S(1)} %get-tuple-element.88.own_ref), channel_id=1, source_target_pairs={{0,1},{1,0},{2,3},{3,2},{4,5},{5,4},{6,7},{7,6},{8,9},{9,8},{10,11... | collective-permute-start | bytes 49160 | tf_op jit(solution)/shard_map/ppermute | solution.py:280
  175.8 10.2 %all_to_all.90.parts_ref = f32[16,24,128]{2,1,0:T(8,128)S(1)} all-to-all(f32[16,24,128]{2,1,0:T(8,128)S(1)} %shard_map.81), channel_id=1, replica_groups=mesh['nodes_0'=4,'nodes_1'=8,'nodes_2'=4,'params'=2] {'nodes_0','nodes_2'}, dimensions={0} | all-to-all | bytes 393216 | tf_op jit(solution)/shard_map/all_to_all | solution.py:276
  186.1 10.0 %all_to_all.91.parts_ref = f32[8,24,128]{2,1,0:T(8,128)S(1)} all-to-all(f32[8,24,128]{2,1,0:T(8,128)S(1)} %shard_map.82), channel_id=1, replica_groups=mesh['nodes_0'=4,'nodes_1'=8,'nodes_2'=4,'params'=2] {'nodes_1'}, dimensions={0} | all-to-all | bytes 196608 | tf_op jit(solution)/shard_map/all_to_all | solution.py:276
  197.6 3.2 %collective-permute-start.8 = (f32[64,1024]{1,0:T(8,128)S(1)}, f32[64,1024]{1,0:T(8,128)S(1)}, u32[]{:S(2)}, u32[]{:S(2)}) collective-permute-start(f32[64,1024]{1,0:T(8,128)S(1)} %get-tuple-element.94.own_ref), channel_id=1, source_target_pairs={{0,1},{1,0},{2,3},{3,2},{4,5},{5,4},{6,7},{7,6},{8,9},{9,8},{10,11... | collective-permute-start | bytes 786440 | tf_op jit(solution)/shard_map/ppermute | solution.py:280
  202.7 2.9 %shard_map.85 = (f32[3072,64]{1,0:T(8,128)S(1)}, f32[16,49,128]{2,1,0:T(8,128)S(1)}) custom-call(bf16[3072,1024]{1,0:T(8,128)(2,1)S(1)} %get-tuple-element.57.rows_ref, f32[64,1024]{1,0:T(8,128)S(1)} %get-tuple-element.94.own_ref, f32[64,1024]{1,0:T(8,128)S(1)} %collective-permute-done.8.other_ref, f32[64,64]{1,0:T(8,128)S(1)} %shard_map.84.inverse_ref, ...), custom_call_target="tpu_custom_call" | custom-call | tf_op jit(solution)/shard_map/pallas_call | solution.py:336
  205.6 13.0 %all_to_all.92.parts_ref = f32[16,49,128]{2,1,0:T(8,128)S(1)} all-to-all(f32[16,49,128]{2,1,0:T(8,128)S(1)} %get-tuple-element.99), channel_id=1, replica_groups=mesh['nodes_0'=4,'nodes_1'=8,'nodes_2'=4,'params'=2] {'nodes_0','nodes_2'}, dimensions={0} | all-to-all | bytes 802816 | tf_op jit(solution)/shard_map/all_to_all | solution.py:276
  218.7 11.8 %all_to_all.93.parts_ref = f32[8,49,128]{2,1,0:T(8,128)S(1)} all-to-all(f32[8,49,128]{2,1,0:T(8,128)S(1)} %shard_map.86), channel_id=1, replica_groups=mesh['nodes_0'=4,'nodes_1'=8,'nodes_2'=4,'params'=2] {'nodes_1'}, dimensions={0} | all-to-all | bytes 401408 | tf_op jit(solution)/shard_map/all_to_all | solution.py:276
  230.5 3.2 %shard_map.87 = (f32[64,64]{1,0:T(8,128)S(1)}, f32[32,128]{1,0:T(8,128)S(1)}, f32[64,64]{1,0:T(8,128)S(1)}) custom-call(f32[8,49,128]{2,1,0:T(8,128)S(1)} %all_to_all.93.parts_ref, f32[64,64]{1,0:T(8,128)S(1)} %get-tuple-element.96.second_ref.time_gram_ref), custom_call_target="tpu_custom_call" | custom-call | tf_op jit(solution)/shard_map/pallas_call | solution.py:324
  233.7 2.8 %collective-permute-start.10 = (f32[32,128]{1,0:T(8,128)S(1)}, f32[32,128]{1,0:T(8,128)S(1)}, u32[]{:S(2)}, u32[]{:S(2)}) collective-permute-start(f32[32,128]{1,0:T(8,128)S(1)} %get-tuple-element.101.own_ref), channel_id=1, source_target_pairs={{0,1},{1,0},{2,3},{3,2},{4,5},{5,4},{6,7},{7,6},{8,9},{9,8},{10,11... | collective-permute-start | bytes 49160 | tf_op jit(solution)/shard_map/ppermute | solution.py:280
  239.3 10.2 %all_to_all.94.parts_ref = f32[16,24,128]{2,1,0:T(8,128)S(1)} all-to-all(f32[16,24,128]{2,1,0:T(8,128)S(1)} %shard_map.90), channel_id=1, replica_groups=mesh['nodes_0'=4,'nodes_1'=8,'nodes_2'=4,'params'=2] {'nodes_0','nodes_2'}, dimensions={0} | all-to-all | bytes 393216 | tf_op jit(solution)/shard_map/all_to_all | solution.py:276
  249.5 10.0 %all_to_all.95.parts_ref = f32[8,24,128]{2,1,0:T(8,128)S(1)} all-to-all(f32[8,24,128]{2,1,0:T(8,128)S(1)} %shard_map.91), channel_id=1, replica_groups=mesh['nodes_0'=4,'nodes_1'=8,'nodes_2'=4,'params'=2] {'nodes_1'}, dimensions={0} | all-to-all | bytes 196608 | tf_op jit(solution)/shard_map/all_to_all | solution.py:276
  261.1 3.0 %collective-permute-start.11 = (f32[64,1024]{1,0:T(8,128)S(1)}, f32[64,1024]{1,0:T(8,128)S(1)}, u32[]{:S(2)}, u32[]{:S(2)}) collective-permute-start(f32[64,1024]{1,0:T(8,128)S(1)} %get-tuple-element.107.own_ref), channel_id=1, source_target_pairs={{0,1},{1,0},{2,3},{3,2},{4,5},{5,4},{6,7},{7,6},{8,9},{9,8},{10,11... | collective-permute-start | bytes 786440 | tf_op jit(solution)/shard_map/ppermute | solution.py:280
  (46 shorter events, 26.9 us)
Async XLA Ops:
  43.5 4.1 %collective-permute-start.1 = (f32[32,128]{1,0:T(8,128)S(1)}, f32[32,128]{1,0:T(8,128)S(1)}, u32[]{:S(2)}, u32[]{:S(2)}) collective-permute-start(f32[32,128]{1,0:T(8,128)S(1)} %get-tuple-element.62.own_ref), channel_id=1, source_target_pairs={{0,1},{1,0},{2,3},{3,2},{4,5},{5,4},{6,7},{7,6},{8,9},{9,8},{10,11... | collective-permute-start | bytes 49160 | tf_op jit(solution)/shard_map/ppermute | solution.py:280
  46.9 2.6 collective-permute-start
  71.2 4.8 %collective-permute-start.2 = (f32[64,1024]{1,0:T(8,128)S(1)}, f32[64,1024]{1,0:T(8,128)S(1)}, u32[]{:S(2)}, u32[]{:S(2)}) collective-permute-start(f32[64,1024]{1,0:T(8,128)S(1)} %get-tuple-element.68.own_ref), channel_id=1, source_target_pairs={{0,1},{1,0},{2,3},{3,2},{4,5},{5,4},{6,7},{7,6},{8,9},{9,8},{10,11... | collective-permute-start | bytes 786440 | tf_op jit(solution)/shard_map/ppermute | solution.py:280
  107.0 3.7 %collective-permute-start.4 = (f32[32,128]{1,0:T(8,128)S(1)}, f32[32,128]{1,0:T(8,128)S(1)}, u32[]{:S(2)}, u32[]{:S(2)}) collective-permute-start(f32[32,128]{1,0:T(8,128)S(1)} %get-tuple-element.75.own_ref), channel_id=1, source_target_pairs={{0,1},{1,0},{2,3},{3,2},{4,5},{5,4},{6,7},{7,6},{8,9},{9,8},{10,11... | collective-permute-start | bytes 49160 | tf_op jit(solution)/shard_map/ppermute | solution.py:280
  110.0 2.6 collective-permute-start.3
  134.4 4.9 %collective-permute-start.5 = (f32[64,1024]{1,0:T(8,128)S(1)}, f32[64,1024]{1,0:T(8,128)S(1)}, u32[]{:S(2)}, u32[]{:S(2)}) collective-permute-start(f32[64,1024]{1,0:T(8,128)S(1)} %get-tuple-element.81.own_ref), channel_id=1, source_target_pairs={{0,1},{1,0},{2,3},{3,2},{4,5},{5,4},{6,7},{7,6},{8,9},{9,8},{10,11... | collective-permute-start | bytes 786440 | tf_op jit(solution)/shard_map/ppermute | solution.py:280
  170.2 3.7 %collective-permute-start.7 = (f32[32,128]{1,0:T(8,128)S(1)}, f32[32,128]{1,0:T(8,128)S(1)}, u32[]{:S(2)}, u32[]{:S(2)}) collective-permute-start(f32[32,128]{1,0:T(8,128)S(1)} %get-tuple-element.88.own_ref), channel_id=1, source_target_pairs={{0,1},{1,0},{2,3},{3,2},{4,5},{5,4},{6,7},{7,6},{8,9},{9,8},{10,11... | collective-permute-start | bytes 49160 | tf_op jit(solution)/shard_map/ppermute | solution.py:280
  173.3 2.6 collective-permute-start.6
  197.6 5.1 %collective-permute-start.8 = (f32[64,1024]{1,0:T(8,128)S(1)}, f32[64,1024]{1,0:T(8,128)S(1)}, u32[]{:S(2)}, u32[]{:S(2)}) collective-permute-start(f32[64,1024]{1,0:T(8,128)S(1)} %get-tuple-element.94.own_ref), channel_id=1, source_target_pairs={{0,1},{1,0},{2,3},{3,2},{4,5},{5,4},{6,7},{7,6},{8,9},{9,8},{10,11... | collective-permute-start | bytes 786440 | tf_op jit(solution)/shard_map/ppermute | solution.py:280
  233.7 3.7 %collective-permute-start.10 = (f32[32,128]{1,0:T(8,128)S(1)}, f32[32,128]{1,0:T(8,128)S(1)}, u32[]{:S(2)}, u32[]{:S(2)}) collective-permute-start(f32[32,128]{1,0:T(8,128)S(1)} %get-tuple-element.101.own_ref), channel_id=1, source_target_pairs={{0,1},{1,0},{2,3},{3,2},{4,5},{5,4},{6,7},{7,6},{8,9},{9,8},{10,11... | collective-permute-start | bytes 49160 | tf_op jit(solution)/shard_map/ppermute | solution.py:280
  236.7 2.6 collective-permute-start.9
  261.1 5.5 %collective-permute-start.11 = (f32[64,1024]{1,0:T(8,128)S(1)}, f32[64,1024]{1,0:T(8,128)S(1)}, u32[]{:S(2)}, u32[]{:S(2)}) collective-permute-start(f32[64,1024]{1,0:T(8,128)S(1)} %get-tuple-element.107.own_ref), channel_id=1, source_target_pairs={{0,1},{1,0},{2,3},{3,2},{4,5},{5,4},{6,7},{7,6},{8,9},{9,8},{10,11... | collective-permute-start | bytes 786440 | tf_op jit(solution)/shard_map/ppermute | solution.py:280
